TPU v7x, 256 devices: a whole 4x4x8 slice. The times are simulated.
256 devices in a mesh: stream: 16 (over y_lo, z), span: 8 (over y_hi, x), rep: 2 (over core).
Axes of the slice: x: 4, y: 4 (y_hi: 2, y_lo: 2; y = y_hi * 2 + y_lo), z: 8, core: 2. Of those that a mesh axis runs over, the one named last changes fastest.
Arguments:
- node_state: bfloat16 [2, 16, 8, 384, 512], P('rep', 'stream', 'span'), may hold values from -6 to 6
- node_cot: bfloat16 [2, 16, 8, 384, 512], P('rep', 'stream', 'span'), may hold values from -6 to 6
- edge_w1: bfloat16 [1, 512, 512], replicated, may hold values from -0.25 to 0.25
- edge_b1: float32 [1, 512], replicated, may hold values from -3 to 3
- edge_w2: bfloat16 [1, 512, 512], replicated, may hold values from -0.25 to 0.25
- node_w1: bfloat16 [1, 1024, 512], replicated, may hold values from -0.1875 to 0.1875
- node_b1: float32 [1, 512], replicated, may hold values from -3 to 3
- node_w2: bfloat16 [1, 512, 512], replicated, may hold values from -0.25 to 0.25
- norm_gain: float32 [1, 512], replicated, may hold values from 0.5 to 1.5
- tile_dst: int32 [16, 8, 24], P('stream', 'span'), may hold values from 0 to 2
- tile_src: int32 [16, 8, 24], P('stream', 'span'), may hold values from 0 to 6, as said below
- tile_count: int32 [16, 8], P('stream', 'span'), may hold values from 6 to 24, as said below
- tile_vals: bfloat16 [16, 8, 24, 128, 128], P('stream', 'span'), may hold values from -0.29882812 to 0.29882812
- send_blocks: int32 [16, 8, 4, 1], P('stream', 'span'), may hold values from 0 to 2
Outputs:
- final_state: bfloat16 [2, 16, 8, 384, 512], P('rep', 'stream', 'span')
- state_grad: bfloat16 [2, 16, 8, 384, 512], P('rep', 'stream', 'span')
- edge_w1_grad: float32 [512, 512], P(('stream', 'span'))
- edge_w2_grad: float32 [512, 512], P(('stream', 'span'))
- node_w1_grad: float32 [1024, 512], P(('stream', 'span'))
- node_w2_grad: float32 [512, 512], P(('stream', 'span'))
Inputs may be any that keep to these rules, and one draw needn't show every extreme that they name: `tile_src`: entries below 3 name own blocks, the others received ones; every received block is named by one of each partition's first 4 slots. `tile_count`: the live slots are the first ones; some partition uses all 24.
All inputs are finite; a program needn't handle non-finite values.
Results may differ from a plain program's by a relative error of at most 0.02.
Values may be sent and summed in bfloat16 or wider, within the bound.
A program may use at most 64 MiB of HBM per device.

v0:
```python
import jax
import jax.numpy as jnp
from jax import lax
from jax.sharding import PartitionSpec as P

norm_epsilon = 1e-05


def with_halo(x, sides, width):
    for axis, dim in sides:
        peers, length = (lax.axis_size(axis), x.shape[dim])
        up = [(i, (i + 1) % peers) for i in range(peers - 1)]
        down = [(j, i) for i, j in up]
        last = lax.slice_in_dim(x, length - width, length, axis=dim)
        first = lax.slice_in_dim(x, 0, width, axis=dim)
        before = lax.ppermute(last, axis, up)
        after = lax.ppermute(first, axis, down)
        x = jnp.concatenate([before, x, after], axis=dim)
    return x


def silu_slope(pre_value):
    logistic = jax.nn.sigmoid(pre_value)
    return logistic * (1.0 + pre_value * (1.0 - logistic))


def matmul(left_op, right_op):
    return jnp.dot(left_op, right_op, preferred_element_type=jnp.float32)


def left_contract(left_op, right_op):
    return lax.dot_general(
        left_op, right_op, (((0,), (0,)), ((), ())), preferred_element_type=jnp.float32
    )


def right_contract(left_op, right_op):
    return lax.dot_general(
        left_op, right_op, (((1,), (1,)), ((), ())), preferred_element_type=jnp.float32
    )


def edge_forward(state_rows, weight_in, bias_in, weight_out):
    pre_act = matmul(state_rows, weight_in) + bias_in
    hidden = jax.nn.silu(pre_act).astype(jnp.bfloat16)
    message = matmul(hidden, weight_out).astype(jnp.bfloat16)
    return (message, pre_act, hidden)


def node_forward(state_rows, gathered, weight_in, bias_in, weight_out, gain_vec):
    feature_width = state_rows.shape[1]
    pre_act = (
        matmul(state_rows, weight_in[:feature_width])
        + matmul(gathered, weight_in[feature_width:])
        + bias_in
    )
    hidden = jax.nn.silu(pre_act).astype(jnp.bfloat16)
    output = matmul(hidden, weight_out)
    centred = output - jnp.mean(output, axis=1, keepdims=True)
    inverse_std = lax.rsqrt(jnp.mean(centred * centred, axis=1, keepdims=True) + norm_epsilon)
    normed = centred * inverse_std
    new_state = (state_rows.astype(jnp.float32) + normed * gain_vec).astype(jnp.bfloat16)
    return (new_state, pre_act, hidden, normed, inverse_std)


def edge_backward(state_rows, pre_act, hidden, weight_in, weight_out, cot_message):
    grad_out = left_contract(hidden, cot_message)
    cot_hidden = right_contract(cot_message, weight_out)
    cot_pre = (cot_hidden * silu_slope(pre_act)).astype(jnp.bfloat16)
    grad_in = left_contract(state_rows, cot_pre)
    cot_state = right_contract(cot_pre, weight_in)
    return (cot_state, grad_in, grad_out)


def node_backward(
    state_rows,
    gathered,
    pre_act,
    hidden,
    normed,
    inverse_std,
    weight_in,
    weight_out,
    gain_vec,
    cot_new,
):
    feature_width = state_rows.shape[1]
    carried = cot_new.astype(jnp.float32)
    scaled = carried * gain_vec
    cot_output = inverse_std * (
        scaled
        - jnp.mean(scaled, axis=1, keepdims=True)
        - normed * jnp.mean(scaled * normed, axis=1, keepdims=True)
    )
    cot_output = cot_output.astype(jnp.bfloat16)
    grad_out = left_contract(hidden, cot_output)
    cot_hidden = right_contract(cot_output, weight_out)
    cot_pre = (cot_hidden * silu_slope(pre_act)).astype(jnp.bfloat16)
    grad_in = jnp.concatenate(
        [left_contract(state_rows, cot_pre), left_contract(gathered, cot_pre)], axis=0
    )
    cot_gathered = right_contract(cot_pre, weight_in[feature_width:]).astype(jnp.bfloat16)
    cot_state = carried + right_contract(cot_pre, weight_in[:feature_width])
    return (cot_state, cot_gathered, grad_in, grad_out)


def send_halo(message_blocks, send_list):
    halo_count = send_list.shape[0] // 4
    block_rows = message_blocks.shape[1]
    feature_width = message_blocks.shape[2]
    picked = jnp.take(message_blocks, send_list, axis=0)
    along = picked[: 2 * halo_count]
    across = picked[2 * halo_count :]
    stream_side = with_halo(along, (("stream", 0),), 1)
    span_side = with_halo(across, (("span", 0),), 1)
    arrived = jnp.concatenate([stream_side[0], stream_side[3], span_side[0], span_side[3]], axis=0)
    arrived = arrived.reshape(4 * halo_count, block_rows, feature_width)
    return jnp.concatenate([message_blocks, arrived], axis=0)


def return_halo(cot_extended, send_list, blocks):
    halo_count = send_list.shape[0] // 4
    block_rows = cot_extended.shape[1]
    feature_width = cot_extended.shape[2]
    outgoing = cot_extended[blocks:].astype(jnp.bfloat16)
    stream_back = with_halo(outgoing[:2], (("stream", 0),), 1)
    span_back = with_halo(outgoing[2:], (("span", 0),), 1)
    returned = jnp.concatenate([stream_back[0], stream_back[3], span_back[0], span_back[3]], axis=0)
    returned = returned.reshape(4 * halo_count, block_rows, feature_width)
    select = (send_list[:, None] == jnp.arange(blocks, dtype=jnp.int32)[None, :]).astype(
        jnp.bfloat16
    )
    added_back = jnp.einsum("jb,jch->bch", select, returned, preferred_element_type=jnp.float32)
    return (cot_extended[:blocks] + added_back).astype(jnp.bfloat16)


def gather_every(extended, values, targets, sources, live_count, blocks):
    slot_count = values.shape[0]
    picked = jnp.take(extended, sources, axis=0)
    products = jnp.einsum("tab,tbh->tah", values, picked, preferred_element_type=jnp.float32)
    live_mask = (jnp.arange(slot_count, dtype=jnp.int32) < live_count).astype(jnp.float32)
    select = (targets[:, None] == jnp.arange(blocks, dtype=jnp.int32)[None, :]).astype(
        jnp.float32
    ) * live_mask[:, None]
    return jnp.einsum("tb,tah->bah", select, products).astype(jnp.bfloat16)


def spread_every(cot_blocks, values, targets, sources, live_count, extent):
    slot_count = values.shape[0]
    picked = jnp.take(cot_blocks, targets, axis=0)
    products = jnp.einsum(
        "tab,tah->tbh", values, picked, preferred_element_type=jnp.float32
    ).astype(jnp.bfloat16)
    live_mask = (jnp.arange(slot_count, dtype=jnp.int32) < live_count).astype(jnp.bfloat16)
    select = (sources[:, None] == jnp.arange(extent, dtype=jnp.int32)[None, :]).astype(
        jnp.bfloat16
    ) * live_mask[:, None]
    return jnp.einsum("te,tah->eah", select, products, preferred_element_type=jnp.float32)


def body(
    node_state,
    node_cot,
    edge_w1,
    edge_b1,
    edge_w2,
    node_w1,
    node_b1,
    node_w2,
    norm_gain,
    tile_dst,
    tile_src,
    tile_count,
    tile_vals,
    send_blocks,
):
    feature_width = node_state.shape[4]
    row_count = node_state.shape[3]
    block_rows = tile_vals.shape[3]
    blocks = row_count // block_rows
    send_list = send_blocks[0, 0].reshape(-1)
    extent = blocks + send_list.shape[0]
    values = tile_vals[0, 0]
    targets = tile_dst[0, 0]
    sources = tile_src[0, 0]
    live_count = tile_count[0, 0]
    state_rows = node_state[0, 0, 0]
    layer_idx = 0
    message, edge_pre, edge_hidden = edge_forward(
        state_rows, edge_w1[layer_idx], edge_b1[layer_idx], edge_w2[layer_idx]
    )
    extended = send_halo(message.reshape(blocks, block_rows, feature_width), send_list)
    gathered = gather_every(extended, values, targets, sources, live_count, blocks)
    gathered = gathered.reshape(row_count, feature_width)
    new_state, node_pre, node_hidden, normed, inverse_std = node_forward(
        state_rows,
        gathered,
        node_w1[layer_idx],
        node_b1[layer_idx],
        node_w2[layer_idx],
        norm_gain[layer_idx],
    )
    stored = [
        (state_rows, edge_pre, edge_hidden, gathered, node_pre, node_hidden, normed, inverse_std)
    ]
    final_state = new_state.reshape(node_state.shape)
    cot_state = node_cot[0, 0, 0]
    grads_e1, grads_e2, grads_n1, grads_n2 = ([], [], [], [])
    layer_idx = 0
    state_in, edge_pre, edge_hidden, gathered, node_pre, node_hidden, normed, inverse_std = stored[
        layer_idx
    ]
    cot_node_state, cot_gathered, grad_n1, grad_n2 = node_backward(
        state_in,
        gathered,
        node_pre,
        node_hidden,
        normed,
        inverse_std,
        node_w1[layer_idx],
        node_w2[layer_idx],
        norm_gain[layer_idx],
        cot_state,
    )
    cot_blocks = cot_gathered.reshape(blocks, block_rows, feature_width)
    cot_extended = spread_every(cot_blocks, values, targets, sources, live_count, extent)
    cot_message = return_halo(cot_extended, send_list, blocks).reshape(row_count, feature_width)
    cot_edge_state, grad_e1, grad_e2 = edge_backward(
        state_in, edge_pre, edge_hidden, edge_w1[layer_idx], edge_w2[layer_idx], cot_message
    )
    cot_state = (cot_node_state + cot_edge_state).astype(jnp.bfloat16)
    grads_e1.insert(0, grad_e1)
    grads_e2.insert(0, grad_e2)
    grads_n1.insert(0, grad_n1)
    grads_n2.insert(0, grad_n2)
    state_grad = cot_state.reshape(node_state.shape)
    local_e1 = grads_e1[0]
    local_e2 = grads_e2[0]
    local_n1 = grads_n1[0]
    local_n2 = grads_n2[0]
    share_e1, share_e2, share_n1, share_n2 = (
        lax.psum_scatter(local_e1, ("stream", "span"), scatter_dimension=0, tiled=True),
        lax.psum_scatter(local_e2, ("stream", "span"), scatter_dimension=0, tiled=True),
        lax.psum_scatter(local_n1, ("stream", "span"), scatter_dimension=0, tiled=True),
        lax.psum_scatter(local_n2, ("stream", "span"), scatter_dimension=0, tiled=True),
    )
    total_e1, total_e2, total_n1, total_n2 = (
        lax.psum(share_e1.astype(jnp.bfloat16), "rep").astype(jnp.float32),
        lax.psum(share_e2.astype(jnp.bfloat16), "rep").astype(jnp.float32),
        lax.psum(share_n1.astype(jnp.bfloat16), "rep").astype(jnp.float32),
        lax.psum(share_n2.astype(jnp.bfloat16), "rep").astype(jnp.float32),
    )
    return (final_state, state_grad, total_e1, total_e2, total_n1, total_n2)


def solution(mesh):
    in_specs = (
        P("rep", "stream", "span", None, None),
        P("rep", "stream", "span", None, None),
        P(),
        P(),
        P(),
        P(),
        P(),
        P(),
        P(),
        P("stream", "span", None),
        P("stream", "span", None),
        P("stream", "span"),
        P("stream", "span", None, None, None),
        P("stream", "span", None, None),
    )
    out_specs = (
        P("rep", "stream", "span", None, None),
        P("rep", "stream", "span", None, None),
        P(("stream", "span"), None),
        P(("stream", "span"), None),
        P(("stream", "span"), None),
        P(("stream", "span"), None),
    )
    return jax.shard_map(body, mesh=mesh, in_specs=in_specs, out_specs=out_specs, check_vma=False)
```

profile of v0, /device:TPU:1, one launch (start us, length us, event | category | flops | bytes accessed | tf_op | source)
XLA Modules:
  0.0 829.4 jit_solution(15360953114151272974)
XLA Ops:
  7.2 0.7 fusion.65
  8.0 0.7 compare_and_fusion.1
  8.6 1.5 convolution_add_fusion.4
  10.2 1.7 convolution_convert_fusion.2
  12.0 0.6 gather_fusion
  12.7 4.4 collective-permute-start
  17.1 1.3 collective-permute-start.1
  18.4 3.1 collective-permute-start.2
  21.5 1.3 collective-permute-start.3
  23.6 1.4 fusion.38
  25.0 0.6 dynamic-slice
  26.3 0.9 collective-permute-done.3
  27.4 2.5 gather_fusion.1
  29.9 4.7 fusion.6
  34.6 4.9 copy.62
  39.5 2.8 convolution_convert_fusion
  42.9 0.5 fusion.76
  43.6 0.5 copy-done.2
  44.5 1.1 fusion.24
  45.6 0.5 fusion.15
  46.1 0.5 fusion.78
  46.6 0.5 convolution_bitcast_fusion
  47.5 1.5 pad_maximum_fusion
  49.0 2.5 gather_fusion.2
  51.6 4.7 convert_bitcast_fusion
  56.2 4.9 copy.65
  61.2 2.7 fusion.77
  63.9 0.9 fusion.74
  64.9 1.3 collective-permute-start.7
  66.2 4.0 collective-permute-start.6
  70.2 1.3 collective-permute-start.5
  71.5 5.0 collective-permute-start.4
  76.5 1.5 fusion.73
  78.0 1.3 convolution_add_fusion.2
  79.7 0.6 fusion.13
  80.5 1.5 fusion.72
  82.0 0.5 fusion.16
  83.0 624.0 %all-reduce.6 = (bf16[512,512]{0,1:T(8,128)(2,1)}, bf16[512,512]{1,0:T(8,128)(2,1)}, bf16[512,512]{1,0:T(8,128)(2,1)}) all-reduce(f32[512,512]{0,1:T(8,128)S(1)} %convolution_bitcast_fusion.1, f32[512,512]{1,0:T(8,128)} %fusion.72, f32[512,512]{1,0:T(8,128)} %fusion.73), channel_id=2, replica_groups=mesh['stream'=16,'span'=8,'rep'=2] {'stream','span'}, use_global_device_ids=true, to_apply=%region_4.5.clone | all-reduce | flops 786432 | bytes 4718592
  707.0 0.7 dynamic-slice_convert_fusion.1
  707.7 0.7 dynamic-slice_convert_fusion.2
  708.4 1.0 dynamic-slice_convert_fusion
  709.4 1.1 fusion.18
  710.6 0.7 convert_element_type.112
  711.3 108.7 %all-reduce.4 = (bf16[4,512]{0,1:T(8,128)(2,1)S(1)}, bf16[4,512]{1,0:T(4,128)(2,1)S(1)}, bf16[8,512]{1,0:T(8,128)(2,1)S(1)}, bf16[4,512]{1,0:T(4,128)(2,1)S(1)}) all-reduce(bf16[4,512]{0,1:T(8,128)(2,1)S(1)} %dynamic-slice_convert_fusion, ...), channel_id=1, replica_groups=mesh['stream'=16,'span'=8,'rep'=2] {'rep'}, use_global_device_ids=true, to_apply=%region_5.6 | all-reduce | flops 10240 | bytes 40960 | tf_op jit(solution)/shard_map/psum | solution.py:248
  820.0 0.6 convert_element_type.113
  820.6 0.6 convert_element_type.111
  821.2 0.6 convert_element_type.115
  821.8 0.7 copy.68
  (75 shorter events, 2.9 us)
Async XLA Ops:
  7.2 22.7 %copy-start = (bf16[1,1,24,128,128]{4,3,2,1,0:T(8,128)(2,1)S(1)}, bf16[1,1,24,128,128]{4,3,2,1,0:T(8,128)(2,1)}, u32[]{:S(2)}) copy-start(bf16[1,1,24,128,128]{4,3,2,1,0:T(8,128)(2,1)} %param.26) | copy-start | bytes 2359300
  7.2 703.4 %reduce-scatter.3.cloned.1.call-start = ((), (), s32[]{:S(2)}) async-start(), calls=%async_computation.1 | async-start | bytes 2113536 | tf_op jit(solution)/shard_map/reduce_scatter | solution.py:244
  10.2 1.8 copy-start.7
  10.2 12.7 %copy-start.15 = (s32[1,1,24]{2,1,0:T(1,128)S(1)}, s32[1,1,24]{2,1,0:T(1,128)}, u32[]{:S(2)}) copy-start(s32[1,1,24]{2,1,0:T(1,128)} %param.24) | copy-start | bytes 292
  10.2 12.7 %copy-start.13 = (s32[1,1,24]{2,1,0:T(1,128)S(1)}, s32[1,1,24]{2,1,0:T(1,128)}, u32[]{:S(2)}) copy-start(s32[1,1,24]{2,1,0:T(1,128)} %param.23) | copy-start | bytes 292
  10.2 13.4 %copy-start.1 = (bf16[1,1,1,384,512]{4,3,2,1,0:T(8,128)(2,1)S(1)}, bf16[1,1,1,384,512]{4,3,2,1,0:T(8,128)(2,1)}, u32[]{:S(2)}) copy-start(bf16[1,1,1,384,512]{4,3,2,1,0:T(8,128)(2,1)} %param.14) | copy-start | bytes 1179652
  11.9 13.0 %copy-start.18 = (u32[256]{0:T(256)S(1)}, u32[256]{0:T(256)}, u32[]{:S(2)}) copy-start(u32[256]{0:T(256)} %constant.69) | copy-start | bytes 3076
  12.7 13.5 %collective-permute-start = (bf16[1,128,512]{2,1,0:T(8,128)(2,1)S(1)}, bf16[1,128,512]{2,1,0:T(8,128)(2,1)S(1)}, u32[]{:S(2)}, u32[]{:S(2)}) collective-permute-start(bf16[1,128,512]{2,1,0:T(8,128)(2,1)S(1)} %get-tuple-element.63), channel_id=1, source_target_pairs={{0,16},{16,32},{32,48},{48,64},{64,80},{80,96},{96,112},{112,128},... | collective-permute-start | bytes 393224 | tf_op jit(solution)/shard_map/ppermute | solution.py:16
  17.1 9.2 %collective-permute-start.1 = (bf16[1,128,512]{2,1,0:T(8,128)(2,1)S(1)}, bf16[1,128,512]{2,1,0:T(8,128)(2,1)S(1)}, u32[]{:S(2)}, u32[]{:S(2)}) collective-permute-start(bf16[1,128,512]{2,1,0:T(8,128)(2,1)S(1)} %get-tuple-element.66), channel_id=1, source_target_pairs={{16,0},{32,16},{48,32},{64,48},{80,64},{96,80},{112,96},{128,112},... | collective-permute-start | bytes 393224 | tf_op jit(solution)/shard_map/ppermute | solution.py:17
  18.4 7.9 collective-permute-start.2
  21.5 5.7 collective-permute-start.3
  39.5 2.9 copy-start.4
  39.5 2.9 copy-start.12
  39.5 3.3 copy-start.16
  42.8 2.8 copy-start.9
  42.9 1.3 copy-start.2
  42.9 1.3 copy-start.11
  61.2 15.3 %copy-start.10 = (f32[384,512]{1,0:T(8,128)S(1)}, f32[384,512]{1,0:T(8,128)}, u32[]{:S(2)}) copy-start(f32[384,512]{1,0:T(8,128)} %copy-done.9) | copy-start | bytes 2359300
  63.9 14.1 %copy-start.5 = (bf16[1,1024,512]{2,1,0:T(8,128)(2,1)S(1)}, bf16[1,1024,512]{2,1,0:T(8,128)(2,1)}, u32[]{:S(2)}) copy-start(bf16[1,1024,512]{2,1,0:T(8,128)(2,1)} %param.19) | copy-start | bytes 3145732
  64.9 14.4 %collective-permute-start.7 = (bf16[1,128,512]{2,0,1:T(2,128)(2,1)S(1)}, bf16[1,128,512]{2,0,1:T(2,128)(2,1)S(1)}, u32[]{:S(2)}, u32[]{:S(2)}) collective-permute-start(bf16[1,128,512]{2,0,1:T(2,128)(2,1)S(1)} %get-tuple-element.58), channel_id=1, source_target_pairs={{2,0},{4,2},{6,4},{8,6},{10,8},{12,10},{14,12},{3,1},{5,3},{7,5},{... | collective-permute-start | bytes 393224 | tf_op jit(solution)/shard_map/ppermute | solution.py:17
  66.2 13.2 %collective-permute-start.6 = (bf16[1,128,512]{2,0,1:T(2,128)(2,1)S(1)}, bf16[1,128,512]{2,0,1:T(2,128)(2,1)S(1)}, u32[]{:S(2)}, u32[]{:S(2)}) collective-permute-start(bf16[1,128,512]{2,0,1:T(2,128)(2,1)S(1)} %get-tuple-element.59), channel_id=1, source_target_pairs={{0,2},{2,4},{4,6},{6,8},{8,10},{10,12},{12,14},{1,3},{3,5},{5,7},{... | collective-permute-start | bytes 393224 | tf_op jit(solution)/shard_map/ppermute | solution.py:16
  70.2 9.2 %collective-permute-start.5 = (bf16[1,128,512]{2,0,1:T(2,128)(2,1)S(1)}, bf16[1,128,512]{2,0,1:T(2,128)(2,1)S(1)}, u32[]{:S(2)}, u32[]{:S(2)}) collective-permute-start(bf16[1,128,512]{2,0,1:T(2,128)(2,1)S(1)} %get-tuple-element.60), channel_id=1, source_target_pairs={{16,0},{32,16},{48,32},{64,48},{80,64},{96,80},{112,96},{128,112},... | collective-permute-start | bytes 393224 | tf_op jit(solution)/shard_map/ppermute | solution.py:17
  71.5 8.1 collective-permute-start.4
  78.0 1.7 copy-start.14
  79.3 1.1 copy-start.8
  80.3 1.7 copy-start.17
  82.5 626.9 %copy-start.3 = (f32[384,512]{1,0:T(8,128)S(1)}, f32[384,512]{1,0:T(8,128)}, u32[]{:S(2)}) copy-start(f32[384,512]{1,0:T(8,128)} %convolution_add_fusion.2) | copy-start | bytes 2359300
  82.9 626.5 %copy-start.6 = (bf16[1,512,512]{2,1,0:T(8,128)(2,1)S(1)}, bf16[1,512,512]{2,1,0:T(8,128)(2,1)}, u32[]{:S(2)}) copy-start(bf16[1,512,512]{2,1,0:T(8,128)(2,1)} %param.16) | copy-start | bytes 1572868
Sparse Core Ops, SparseCore 0:
  49.1 611.6 reduce-scatter.2
where the time goes:
time: 845 us; the launch traced here: 829 us
  blocking collectives  733 us (87%)
  matrix products  29.2 us (3%)
  starting transfers between devices  21.7 us (3%)
  local copies, waits for them, and re-layouts  21.2 us (3%)
  between operations  15.9 us (2%)
    unnamed x1, blocking collectives  624 us
    psum x1, blocking collectives, body(): lax.psum(share_e1.astype(jnp.bfloat16), 'rep').astype(jnp.float32)  109 us
  transfers between devices with their start and end apart: 9, of which 2 were waited for; matrix products, arithmetic and copies ran while one was open for 3% of the time, Pallas kernels for 0%

commit v1 on v0

v1 whole, which is shorter than its diff:
```python
import functools

import jax
import jax.numpy as jnp
from jax import lax
from jax.experimental import pallas as pl
from jax.experimental.pallas import tpu as pltpu
from jax.sharding import PartitionSpec as P

norm_epsilon = 1e-05
f32, bf16, i32 = jnp.float32, jnp.bfloat16, jnp.int32
MESH = pl.DeviceIdType.MESH
Y_LO = 2
Y_HI = 2
BLK = 3
EXTENT = 7


def log2(n):
    assert n & (n - 1) == 0
    return n.bit_length() - 1


def mm(left_op, right_op):
    return jnp.dot(left_op, right_op, preferred_element_type=f32)


def nt(left_op, right_op):
    return lax.dot_general(left_op, right_op, (((1,), (1,)), ((), ())), preferred_element_type=f32)


def loop(total, step, fn):
    def trip(i, carry):
        fn(pl.multiple_of(i * step, step))
        return carry

    lax.fori_loop(0, total // step, trip, 0)


def kernel(
    Z, X, H, B, T,
    dst_s, src_s, cnt_s, snd_s,
    eb1, nb1, gain,
    st_h, ct_h, ew1_h, ew2_h, nw1_h, nw2_h, vals_h,
    fs_h, sg_h, ge1, ge2, gn1, gn2,
    st, ct, ew1, ew2, nw1, nw2, vals, in_sem,
    slope, hid, msg, ext, sendb, mask, amat, amat_t, p4a, p4b, p8,
    he_t, s4_t, sg8_t, hn_t, part, gath, cot_out, cot_pre, cot_g, csp, own, tmp, tmp2, fsv,
    rets, ret, cot_msg, cot_pre_e,
    n_keep, n_r0s, n_r0, n_s1s, n_s1, n_s2s, n_s2, n_s3s, n_s3, n_fs, n_f,
    e_keep, e_r0s, e_r0, e_s1s, e_s1, e_s2s, e_s2, e_s3s, e_s3, e_fs, e_f,
    halo_ss, halo_rs, ret_ss, ret_rs, n_ss, n_rs, e_ss, e_rs, out_sem,
):
    R = BLK * B
    HC = H // 2
    Y = Y_LO * Y_HI
    SHARDS = Z * X * Y
    K4 = H // SHARDS
    s = lax.axis_index("stream")
    p = lax.axis_index("span")
    r = lax.axis_index("rep")
    y_lo, z = s // Z, s % Z
    y_hi, x = p // X, p % X
    y = y_hi * Y_LO + y_lo
    first = r == 0
    a = jnp.where(first, y, x)
    b = jnp.where(first, x, y)
    has = (s > 0, s < Y_LO * Z - 1, p > 0, p < Y_HI * X - 1)

    def at(yy, xx, zz):
        return {"stream": (yy % Y_LO) * Z + zz, "span": (yy // Y_LO) * X + xx, "rep": r}

    def a_peer(j):
        return at(jnp.where(first, (y + j) % Y, y), jnp.where(first, x, (x + j) % X), z)

    def b_peer(j):
        return at(jnp.where(first, y, (y + j) % Y), jnp.where(first, (x + j) % X, x), z)

    def z_peer(j):
        return at(y, x, (z + j) % Z)

    partner = {"stream": s, "span": p, "rep": 1 - r}
    sides = (
        {"stream": s - 1, "span": p, "rep": r},
        {"stream": s + 1, "span": p, "rep": r},
        {"stream": s, "span": p - 1, "rep": r},
        {"stream": s, "span": p + 1, "rep": r},
    )

    def remote(src, dst, ssem, rsem, dev):
        return pltpu.make_async_remote_copy(
            src_ref=src, dst_ref=dst, send_sem=ssem, recv_sem=rsem, device_id=dev, device_id_type=MESH
        )

    barrier = pltpu.get_barrier_semaphore()
    peers = [partner] + [a_peer(j) for j in range(1, 4)] + [b_peer(j) for j in range(1, 4)]
    peers += [z_peer(j) for j in range(1, Z)]
    for dev in peers:
        pl.semaphore_signal(barrier, inc=1, device_id=dev, device_id_type=MESH)
    halo_count = 0
    for side in range(4):
        halo_count = halo_count + has[side].astype(i32)

        @pl.when(has[side])
        def _():
            pl.semaphore_signal(barrier, inc=1, device_id=sides[side], device_id_type=MESH)

    loads = [
        pltpu.make_async_copy(src, dst, in_sem.at[i])
        for i, (src, dst) in enumerate(
            ((st_h, st), (ew1_h, ew1), (ew2_h, ew2), (vals_h, vals), (nw1_h, nw1), (nw2_h, nw2), (ct_h, ct))
        )
    ]
    for copy in loads:
        copy.start()

    CH = min(32, B)
    loads[0].wait()
    loads[1].wait()
    tmp[...] = mm(st[...], ew1[...])

    def edge_act(i):
        rows = pl.ds(i, CH)
        pre = tmp[rows, :] + eb1[...]
        g = jax.nn.sigmoid(pre)
        hid[rows, :] = (pre * g).astype(bf16)
        slope[rows, :] = g * (1.0 + pre * (1.0 - g))

    loop(R, CH, edge_act)
    loads[2].wait()
    tmp[...] = mm(hid[...], ew2[...])
    for blk in range(BLK):
        msg[blk] = tmp[blk * B : (blk + 1) * B, :].astype(bf16)
    for j in range(4):
        sendb[j] = msg[snd_s[j]]
    pl.semaphore_wait(barrier, len(peers) + halo_count)

    back = (1, 0, 3, 2)
    halo = [
        remote(sendb.at[j], ext.at[back[j]], halo_ss.at[j], halo_rs.at[back[j]], sides[j]) for j in range(4)
    ]
    for j in range(4):

        @pl.when(has[j])
        def _():
            halo[j].start()

        @pl.when(jnp.logical_not(has[j]))
        def _():
            ext[j] = jnp.zeros((B, H), bf16)
            ret[j] = jnp.zeros((B, H), bf16)

    def masks(t, carry):
        key = jnp.where(t < cnt_s[0], dst_s[t] * EXTENT + src_s[t], -1)
        keys = jnp.full((8, B), key, i32)
        for q in range(BLK * EXTENT):
            mask[t, q] = jnp.where(keys == q, 1.0, 0.0).astype(f32)
        return carry

    lax.fori_loop(0, T, masks, 0)
    loads[3].wait()

    def tiles(i):
        totals = [[jnp.zeros((8, B), f32)] * 2 for _ in range(BLK * EXTENT)]
        for t in range(T):
            v = vals[t, pl.ds(i, 16), :].astype(f32)
            halves = (v[:8], v[8:])
            for q in range(BLK * EXTENT):
                m = mask[t, q]
                totals[q] = [totals[q][0] + m * halves[0], totals[q][1] + m * halves[1]]
        for q in range(BLK * EXTENT):
            d, e = q // EXTENT, q % EXTENT
            amat[pl.ds(pl.multiple_of(d * B + i, 16), 16), e * B : (e + 1) * B] = jnp.concatenate(
                totals[q], axis=0
            ).astype(bf16)

    loop(B, 16, tiles)
    eye = (lax.broadcasted_iota(i32, (B, B), 0) == lax.broadcasted_iota(i32, (B, B), 1)).astype(f32).astype(bf16)
    for e in range(EXTENT):
        amat_t[e * B : (e + 1) * B, :] = nt(eye, amat[:, e * B : (e + 1) * B]).astype(bf16)

    lk, lz, lx, ly = log2(K4), log2(Z), log2(X), log2(Y)

    def row_of(k, zz, bb, aa, k_bits):
        yy = jnp.where(first, aa, bb)
        xx = jnp.where(first, bb, aa)
        per = 1 << k_bits
        return (
            (yy & 1) * (per * X * Y_HI * Z) + zz * (per * X * Y_HI) + (yy >> 1) * (per * X) + xx * per + k
        )

    LW = min(128, H)

    def perms(i):
        pos = i + lax.broadcasted_iota(i32, (CH, LW), 0)
        lane = lax.broadcasted_iota(i32, (CH, LW), 1)
        k = pos & (K4 - 1)
        half = (pos >> lk) & 1
        zp = (pos >> (lk + 1)) & (Z // 2 - 1)
        bb = (pos >> (lk + lz)) & 3
        aa = (pos >> (lk + lz + 2)) & 3
        rows = pl.ds(i, CH)
        for ref, zz in ((p4a, 2 * zp + half), (p4b, 2 * zp + 1 - half)):
            orig = row_of(k, zz, bb, aa, lk)
            for c in range(H // LW):
                ref[rows, c * LW : (c + 1) * LW] = jnp.where(orig == lane + c * LW, 1.0, 0.0).astype(bf16)

    loop(H, CH, perms)

    def perms8(i):
        pos = i + lax.broadcasted_iota(i32, (CH, LW), 0)
        lane = lax.broadcasted_iota(i32, (CH, LW), 1)
        k = pos & (2 * K4 - 1)
        zz = (pos >> (lk + 1)) & (Z - 1)
        bb = (pos >> (lk + 1 + lz)) & 3
        aa = (pos >> (lk + 3 + lz)) & 3
        orig = row_of(k, zz, bb, aa, lk + 1)
        for c in range(2 * H // LW):
            p8[pl.ds(i, CH), c * LW : (c + 1) * LW] = jnp.where(orig == lane + c * LW, 1.0, 0.0).astype(bf16)

    loop(2 * H, CH, perms8)
    s4_t[...] = nt(p4a[...], st[...]).astype(bf16)
    he_t[...] = nt(p4b[...], hid[...]).astype(bf16)
    tmp2[...] = nt(p8[:, :H], st[...])
    loads[4].wait()
    part[...] = mm(st[...], nw1[:H, :])
    own[...] = mm(amat[:, :R], msg[...].reshape(R, H))
    loads[5].wait()
    loads[6].wait()

    for j in range(4):

        @pl.when(has[j])
        def _():
            halo[back[j]].wait_recv()

    gath[...] = (own[...] + mm(amat[:, R:], ext[...].reshape(4 * B, H))).astype(bf16)
    part[...] += mm(gath[...], nw1[H:, :])

    def node_act(i):
        rows = pl.ds(i, CH)
        pre = part[rows, :] + nb1[...]
        g = jax.nn.sigmoid(pre)
        hid[rows, :] = (pre * g).astype(bf16)
        part[rows, :] = g * (1.0 + pre * (1.0 - g))

    loop(R, CH, node_act)
    tmp[...] = mm(hid[...], nw2[...])

    def norm(i):
        rows = pl.ds(i, CH)
        o = tmp[rows, :]
        centred = o - jnp.mean(o, axis=1, keepdims=True)
        inv = lax.rsqrt(jnp.mean(centred * centred, axis=1, keepdims=True) + norm_epsilon)
        normed = centred * inv
        fsv[rows, :] = (st[rows, :].astype(f32) + normed * gain[...]).astype(bf16)
        q = ct[rows, :].astype(f32) * gain[...]
        cot = inv * (
            q - jnp.mean(q, axis=1, keepdims=True) - normed * jnp.mean(q * normed, axis=1, keepdims=True)
        )
        cot_out[rows, :] = cot.astype(bf16)

    loop(R, CH, norm)
    out_fs = pltpu.make_async_copy(fsv, fs_h, out_sem.at[0])
    out_fs.start()
    tmp[...] = nt(cot_out[...], nw2[...])

    def node_slope(i):
        rows = pl.ds(i, CH)
        cot_pre[rows, :] = (tmp[rows, :] * part[rows, :]).astype(bf16)

    loop(R, CH, node_slope)
    cot_g[...] = nt(cot_pre[...], nw1[H:, :]).astype(bf16)

    rets[...] = mm(amat_t[R:, :], cot_g[...]).astype(bf16).reshape(4, B, H)
    home = [
        remote(rets.at[g], ret.at[back[g]], ret_ss.at[g], ret_rs.at[back[g]], sides[g]) for g in range(4)
    ]
    for g in range(4):

        @pl.when(has[g])
        def _():
            home[g].start()

    def halves(base, size, i, left, right):
        block = size // 4
        n_keep[pl.ds(pl.multiple_of(base + i, size), size), :] = jnp.where(first, left, right)
        sent = jnp.where(first, right, left).astype(bf16)
        for bb in range(4):
            rows = pl.ds(pl.multiple_of(base + bb * size + i // 4, block), block)
            n_r0s[rows, :] = sent[bb * block : (bb + 1) * block]

    hn_t[...] = nt(p4a[...], hid[...]).astype(bf16)
    sg8_t[...] = (tmp2[...] + nt(p8[:, H:], gath[...])).astype(bf16)
    own[...] = mm(amat_t[:R, :], cot_g[...])

    def grad_rows(base, size, left_ref, right_ref):
        def go(i):
            g = mm(left_ref[pl.ds(i, size), :], right_ref[...])
            halves(base, size, i, g[:, :HC], g[:, HC:])

        return go

    n1_rows, n2_rows = 2 * H // Y, H // Y
    loop(2 * H, n1_rows, grad_rows(0, n1_rows, sg8_t, cot_pre))
    loop(H, n2_rows, grad_rows(2 * H, n2_rows, hn_t, cot_out))
    n_rep = remote(n_r0s, n_r0, n_ss.at[0], n_rs.at[0], partner)
    n_rep.start()
    csp[...] = nt(cot_pre[...], nw1[:H, :])

    for j in range(4):

        @pl.when(has[j])
        def _():
            home[back[j]].wait_recv()

    def fold(i):
        rows = pl.ds(i, CH)
        for blk in range(BLK):
            full = pl.ds(pl.multiple_of(blk * B + i, CH), CH)
            total = own[full, :]
            for j in range(4):
                total = total + jnp.where(snd_s[j] == blk, ret[j, rows, :].astype(f32), 0.0)
            cot_msg[full, :] = total.astype(bf16)

    loop(B, CH, fold)

    tmp[...] = nt(cot_msg[...], ew2[...])

    def edge_slope(i):
        rows = pl.ds(i, CH)
        cot_pre_e[rows, :] = (tmp[rows, :] * slope[rows, :]).astype(bf16)

    loop(R, CH, edge_slope)

    def spread_stage(send, recv, ssem, rsem, base, me, count, peer):
        copies = []
        for j in range(1, count):
            copies.append(
                remote(
                    send.at[(me + j) % count], recv.at[j - 1], ssem.at[base + j - 1], rsem.at[base + j - 1], peer(j)
                )
            )
        return copies

    def gathered_sum(send, recv, me, count, rows):
        total = send[me, rows, :].astype(f32)
        for j in range(count - 1):
            total = total + recv[j, rows, :].astype(f32)
        return total

    n_rep.wait_recv()

    def n_first(i):
        for aa in range(Y):
            for base, size, off in ((0, n1_rows, 0), (2 * H, n2_rows, n1_rows)):
                step = size // 4
                rows = pl.ds(pl.multiple_of(base + aa * size + i * step, step), step)
                n_s1s[aa, pl.ds(pl.multiple_of(off + i * step, step), step), :] = (
                    n_keep[rows, :] + n_r0[rows, :].astype(f32)
                ).astype(bf16)

    lax.fori_loop(0, 4, lambda i, c: (n_first(i), c)[1], 0)
    n1 = spread_stage(n_s1s, n_s1, n_ss, n_rs, 1, a, Y, a_peer)
    for copy in n1:
        copy.start()

    sub = H // Y

    def e_grad(i):
        rows = pl.ds(i, sub)
        ga = mm(s4_t[rows, :], cot_pre_e[...])
        gb = mm(he_t[rows, :], cot_msg[...])
        lo = (lax.broadcasted_iota(i32, (sub, HC), 0) & (2 * K4 - 1)) < K4
        out = pl.multiple_of(2 * i, 2 * sub)
        for half in range(2):
            u, v = (ga, gb) if half == 0 else (gb, ga)
            left = jnp.where(lo, u[:, :HC], v[:, :HC])
            right = jnp.where(lo, u[:, HC:], v[:, HC:])
            at_rows = pl.ds(pl.multiple_of(out + half * sub, sub), sub)
            e_keep[at_rows, :] = jnp.where(first, left, right)
            sent = jnp.where(first, right, left).astype(bf16)
            block = sub // 4
            for bb in range(4):
                there = pl.ds(pl.multiple_of((2 * bb + half) * sub + i // 4, block), block)
                e_r0s[there, :] = sent[bb * block : (bb + 1) * block]

    loop(H, sub, e_grad)
    e_rep = remote(e_r0s, e_r0, e_ss.at[0], e_rs.at[0], partner)
    e_rep.start()

    csp[...] += nt(cot_pre_e[...], ew1[...])

    def finish_state(i):
        rows = pl.ds(i, CH)
        fsv2 = ct[rows, :].astype(f32) + csp[rows, :]
        ct[rows, :] = fsv2.astype(bf16)

    loop(R, CH, finish_state)
    out_sg = pltpu.make_async_copy(ct, sg_h, out_sem.at[1])
    out_sg.start()

    e_rep.wait_recv()

    def e_first(i):
        rows = pl.ds(i, sub)
        for aa in range(Y):
            full = pl.ds(pl.multiple_of(aa * 2 * sub + i, sub), sub)
            e_s1s[aa, rows, :] = (e_keep[full, :] + e_r0[full, :].astype(f32)).astype(bf16)

    loop(2 * sub, sub, e_first)
    e1 = spread_stage(e_s1s, e_s1, e_ss, e_rs, 1, a, Y, a_peer)
    for copy in e1:
        copy.start()

    for copy in n1:
        copy.wait_recv()
    zs = 2 * K4 * Z
    zh = K4 * Z
    for bb in range(X):
        n_s2s[bb, :zs, :] = gathered_sum(n_s1s, n_s1, a, Y, pl.ds(bb * zs, zs)).astype(bf16)
        n_s2s[bb, zs:, :] = gathered_sum(n_s1s, n_s1, a, Y, pl.ds(n1_rows + bb * zh, zh)).astype(bf16)
    n2 = spread_stage(n_s2s, n_s2, n_ss, n_rs, 4, b, X, b_peer)
    for copy in n2:
        copy.start()
    for copy in e1:
        copy.wait_recv()
    for bb in range(X):
        for half in range(2):
            e_s2s[bb, half * zh : (half + 1) * zh, :] = gathered_sum(
                e_s1s, e_s1, a, Y, pl.ds(half * sub + bb * zh, zh)
            ).astype(bf16)
    e2 = spread_stage(e_s2s, e_s2, e_ss, e_rs, 4, b, X, b_peer)
    for copy in e2:
        copy.start()

    k8 = 2 * K4
    for copy in n2:
        copy.wait_recv()
    nt_rows = gathered_sum(n_s2s, n_s2, b, X, pl.ds(0, zs + zh))
    for zz in range(Z):
        n_s3s[zz] = jnp.concatenate(
            [nt_rows[zz * k8 : (zz + 1) * k8], nt_rows[zs + (zz // 2) * k8 : zs + (zz // 2 + 1) * k8]], axis=0
        ).astype(bf16)
    n3 = spread_stage(n_s3s, n_s3, n_ss, n_rs, 7, z, Z, z_peer)
    for copy in n3:
        copy.start()
    for copy in e2:
        copy.wait_recv()
    et_rows = gathered_sum(e_s2s, e_s2, b, X, pl.ds(0, 2 * zh))
    for zz in range(Z):
        at_row = (zz % 2) * zh + (zz // 2) * k8
        e_s3s[zz] = et_rows[at_row : at_row + k8].astype(bf16)
    e3 = spread_stage(e_s3s, e_s3, e_ss, e_rs, 7, z, Z, z_peer)
    for copy in e3:
        copy.start()

    for copy in n3:
        copy.wait_recv()
    n_fs[...] = gathered_sum(n_s3s, n_s3, z, Z, pl.ds(0, 2 * k8))
    last = 6 + Z
    n_fin = remote(n_fs, n_f, n_ss.at[last], n_rs.at[last], partner)
    n_fin.start()
    for copy in e3:
        copy.wait_recv()
    e_fs[...] = gathered_sum(e_s3s, e_s3, z, Z, pl.ds(0, k8))
    e_fin = remote(e_fs, e_f, e_ss.at[last], e_rs.at[last], partner)
    e_fin.start()

    odd = (z % 2) == 1

    def whole(mine, theirs):
        u, v = mine[...], theirs[...]
        return jnp.concatenate([jnp.where(first, u, v), jnp.where(first, v, u)], axis=1)

    n_fin.wait_recv()
    full = whole(n_fs, n_f)
    gn1[...] = full[:k8]
    gn2[...] = jnp.where(odd, full[k8 + K4 :], full[k8 : k8 + K4])
    e_fin.wait_recv()
    full = whole(e_fs, e_f)
    ge1[...] = jnp.where(odd, full[K4:], full[:K4])
    ge2[...] = jnp.where(odd, full[:K4], full[K4:])

    out_fs.wait()
    out_sg.wait()
    for j in range(4):

        @pl.when(has[j])
        def _():
            halo[j].wait_send()
            home[j].wait_send()

    for copy in [n_rep, e_rep, n_fin, e_fin] + n1 + n2 + n3 + e1 + e2 + e3:
        copy.wait_send()


def make_body(Z, X):
    def body(
        node_state, node_cot, edge_w1, edge_b1, edge_w2, node_w1, node_b1, node_w2, norm_gain,
        tile_dst, tile_src, tile_count, tile_vals, send_blocks,
    ):
        R, H = node_state.shape[3:]
        T, B = tile_vals.shape[2:4]
        Y = Y_LO * Y_HI
        HC = H // 2
        K4 = H // (Z * X * Y)
        k8 = 2 * K4

        def v(shape, dtype=bf16):
            return pltpu.VMEM(shape, dtype)

        def stages(total, s1, s2, s3):
            return [
                v((total, HC), f32), v((total, HC)), v((total, HC)),
                v((Y, s1, HC)), v((Y - 1, s1, HC)),
                v((X, s2, HC)), v((X - 1, s2, HC)),
                v((Z, s3, HC)), v((Z - 1, s3, HC)),
                v((s3, HC), f32), v((s3, HC), f32),
            ]

        dma = pltpu.SemaphoreType.DMA
        scratch = [
            v((R, H)), v((R, H)), v((H, H)), v((H, H)), v((2 * H, H)), v((H, H)), v((T, B, B)), dma((7,)),
            v((R, H), f32), v((R, H)), v((BLK, B, H)), v((4, B, H)), v((4, B, H)), v((T, BLK * EXTENT, 8, B), f32),
            v((R, EXTENT * B)), v((EXTENT * B, R)), v((H, H)), v((H, H)), v((2 * H, 2 * H)),
            v((H, R)), v((H, R)), v((2 * H, R)), v((H, R)), v((R, H), f32), v((R, H)), v((R, H)), v((R, H)),
            v((R, H)), v((R, H), f32), v((R, H), f32), v((R, H), f32), v((2 * H, R), f32), v((R, H)),
            v((4, B, H)), v((4, B, H)), v((R, H)), v((R, H)),
        ]
        scratch += stages(3 * H, 3 * H // Y, 3 * H // (Y * X), 2 * k8)
        scratch += stages(2 * H, 2 * H // Y, 2 * H // (Y * X), k8)
        count = 7 + Z
        scratch += [dma((4,)), dma((4,)), dma((4,)), dma((4,))] + [dma((count,))] * 4 + [dma((2,))]
        smem = pl.BlockSpec(memory_space=pltpu.SMEM)
        vmem = pl.BlockSpec(memory_space=pltpu.VMEM)
        hbm = pl.BlockSpec(memory_space=pl.ANY)
        outs = pl.pallas_call(
            functools.partial(kernel, Z, X, H, B, T),
            out_shape=(
                jax.ShapeDtypeStruct((R, H), bf16),
                jax.ShapeDtypeStruct((R, H), bf16),
                jax.ShapeDtypeStruct((K4, H), f32),
                jax.ShapeDtypeStruct((K4, H), f32),
                jax.ShapeDtypeStruct((k8, H), f32),
                jax.ShapeDtypeStruct((K4, H), f32),
            ),
            in_specs=[smem] * 4 + [vmem] * 3 + [hbm] * 7,
            out_specs=[hbm] * 2 + [vmem] * 4,
            scratch_shapes=scratch,
            compiler_params=pltpu.CompilerParams(
                collective_id=0, has_side_effects=True, vmem_limit_bytes=60 * 1024 * 1024
            ),
            name="step",
        )(
            tile_dst.reshape(T), tile_src.reshape(T), tile_count.reshape(1), send_blocks.reshape(4),
            edge_b1.reshape(1, H), node_b1.reshape(1, H), norm_gain.reshape(1, H),
            node_state.reshape(R, H), node_cot.reshape(R, H), edge_w1.reshape(H, H), edge_w2.reshape(H, H),
            node_w1.reshape(2 * H, H), node_w2.reshape(H, H), tile_vals.reshape(T, B, B),
        )
        return (outs[0].reshape(node_state.shape), outs[1].reshape(node_state.shape)) + tuple(outs[2:])

    return body


def solution(mesh):
    in_specs = (
        P("rep", "stream", "span", None, None),
        P("rep", "stream", "span", None, None),
        P(), P(), P(), P(), P(), P(), P(),
        P("stream", "span", None),
        P("stream", "span", None),
        P("stream", "span"),
        P("stream", "span", None, None, None),
        P("stream", "span", None, None),
    )
    out_specs = (
        P("rep", "stream", "span", None, None),
        P("rep", "stream", "span", None, None),
        P(("stream", "span"), None),
        P(("stream", "span"), None),
        P(("stream", "span"), None),
        P(("stream", "span"), None),
    )
    body = make_body(mesh.shape["stream"] // Y_LO, mesh.shape["span"] // Y_HI)
    return jax.shard_map(body, mesh=mesh, in_specs=in_specs, out_specs=out_specs, check_vma=False)
```

time: 845 us -> 61.1 us (0.07); the launches traced: 829 us -> 60.9 us
  blocking collectives: 733 us -> 0 us
  Pallas kernels: 0 us -> 54.6 us
  matrix products: 29.2 us -> 0 us
  starting transfers between devices: 21.7 us -> 0 us
  local copies, waits for them, and re-layouts: 21.2 us -> 5.08 us
  between operations: 15.9 us -> 1.31 us
    unnamed x1 -> x0, blocking collectives: 624 us -> none
    psum x1 -> x0, blocking collectives: 109 us -> none  [body(): lax.psum(share_e1.astype(jnp.bfloat16), 'rep').astype(jnp.float32)]
    pallas_call x0 -> x1, Pallas kernels: none -> 54.6 us  [body(): pl.pallas_call(functools.partial(kernel, Z, X, H, B, T), out_shape=(jax.S...]
    dot_general x20 -> x0, matrix products: 29.2 us -> none  [the longest x5 5.5 us: matmul(): return jnp.dot(left_op, right_op, preferred_element_type=jnp.float32)]
    ppermute x8 -> x0, starting transfers between devices: 21.7 us -> none  [the longest x4 16.5 us: with_halo(): before = lax.ppermute(last, axis, up)]
  transfers between devices with their start and end apart: 9 -> 0, of which waited for: 2 -> 0; matrix products, arithmetic and copies ran while one was open for 3% -> 0% of each run, Pallas kernels for 0% -> 0%
where the time goes in v1:
time: 61.1 us; the launch traced here: 60.9 us
  Pallas kernels  54.6 us (89%)
  local copies, waits for them, and re-layouts  5.08 us (8%)
  between operations  1.31 us (2%)
    pallas_call x1, Pallas kernels, body(): pl.pallas_call(functools.partial(kernel, Z, X, H, B, T), out_shape=(jax.S...  54.6 us
    unnamed x16, local copies, waits for them, and re-layouts  5.08 us

profile of v1, /device:TPU:1, one launch (start us, length us, event | category | flops | bytes accessed | tf_op | source)
XLA Modules:
  0.0 60.9 jit_solution(149636218513309713)
XLA Ops:
  1.3 54.6 %step.1 = (bf16[384,512]{1,0:T(8,128)(2,1)}, bf16[384,512]{1,0:T(8,128)(2,1)}, f32[4,512]{1,0:T(4,128)}, f32[4,512]{1,0:T(4,128)}, f32[8,512]{1,0:T(8,128)}, /*index=5*/f32[4,512]{1,0:T(4,128)}) custom-call(s32[24]{0:T(128)} %bitcast.23, s32[24]{0:T(128)} %bitcast.24, s32[1]{0:T(128)} %bitcast.13.cnt_s, s32[4]{0:T(128)} %bitcast.25, f32[1,512]{1,0:T(1,128)} %eb1.1, ...), custom_call_target="tpu_custom_call" | custom-call | tf_op jit(solution)/shard_map/step/pallas_call | solution.py:538
  55.9 0.0 copy-start
  55.9 1.8 %copy.27 = bf16[1,1,1,384,512]{4,3,2,1,0:T(8,128)(2,1)} copy(bf16[1,1,1,384,512]{4,3,2,1,0:T(8,128)(2,1)} %bitcast.22) | data formatting | bytes 786432
  57.7 0.0 copy-done
  57.7 0.0 copy-start.4
  57.7 0.0 copy-start.3
  57.7 0.7 %copy.28 = bf16[1,1,1,384,512]{4,3,2,1,0:T(8,128)(2,1)} copy(bf16[1,1,1,384,512]{4,3,2,1,0:T(8,128)(2,1)S(1)} %bitcast.21) | data formatting | bytes 786432
  58.4 0.0 copy-done.4
  58.4 0.0 copy-start.1
  58.4 0.6 copy.29
  59.0 0.0 copy-done.3
  59.0 0.6 copy.30
  59.6 0.0 copy-done.1
  59.6 0.0 copy-start.2
  59.6 0.6 copy.31
  60.3 0.1 copy-done.2
  60.4 0.6 copy.32
Async XLA Ops:
  55.9 1.8 %copy-start = (bf16[384,512]{1,0:T(8,128)(2,1)S(1)}, bf16[384,512]{1,0:T(8,128)(2,1)}, u32[]{:S(2)}) copy-start(bf16[384,512]{1,0:T(8,128)(2,1)} %get-tuple-element.13) | copy-start | bytes 1179652
  57.7 0.8 %copy-start.4 = (f32[4,512]{1,0:T(4,128)S(1)}, f32[4,512]{1,0:T(4,128)}, u32[]{:S(2)}) copy-start(f32[4,512]{1,0:T(4,128)} %get-tuple-element.26) | copy-start | bytes 24580
  57.7 1.4 %copy-start.3 = (f32[4,512]{1,0:T(4,128)S(1)}, f32[4,512]{1,0:T(4,128)}, u32[]{:S(2)}) copy-start(f32[4,512]{1,0:T(4,128)} %get-tuple-element.27) | copy-start | bytes 24580
  58.4 1.2 %copy-start.1 = (f32[8,512]{1,0:T(8,128)S(1)}, f32[8,512]{1,0:T(8,128)}, u32[]{:S(2)}) copy-start(f32[8,512]{1,0:T(8,128)} %get-tuple-element.28) | copy-start | bytes 49156
  59.6 0.7 %copy-start.2 = (f32[4,512]{1,0:T(4,128)S(1)}, f32[4,512]{1,0:T(4,128)}, u32[]{:S(2)}) copy-start(f32[4,512]{1,0:T(4,128)} %get-tuple-element.29) | copy-start | bytes 24580

commit v2 on v1

v2 whole, which is shorter than its diff:
```python
import functools

import jax
import jax.numpy as jnp
from jax import lax
from jax.experimental import pallas as pl
from jax.experimental.pallas import tpu as pltpu
from jax.sharding import PartitionSpec as P

norm_epsilon = 1e-05
f32, bf16, i32 = jnp.float32, jnp.bfloat16, jnp.int32
MESH = pl.DeviceIdType.MESH
Y_LO = 2
Y_HI = 2
BLK = 3
EXTENT = 7


def log2(n):
    assert n & (n - 1) == 0
    return n.bit_length() - 1


def mm(left_op, right_op):
    return jnp.dot(left_op, right_op, preferred_element_type=f32)


def nt(left_op, right_op):
    return lax.dot_general(left_op, right_op, (((1,), (1,)), ((), ())), preferred_element_type=f32)


def unrolled(total, step, fn):
    for i in range(0, total, step):
        fn(i)


def loop(total, step, fn):
    def trip(i, carry):
        fn(pl.multiple_of(i * step, step))
        return carry

    lax.fori_loop(0, total // step, trip, 0)


def kernel(
    Z, X, H, B, T,
    dst_h, src_h, cnt_h, snd_h, eb1_h, nb1_h, gain_h,
    st_h, ct_h, ew1_h, ew2_h, nw1_h, nw2_h, vals_h,
    states_h, grads,
    dst_s, src_s, cnt_s, snd_s, eb1, nb1, gain,
    st, ct, ew1, ew2, nw1, nw2, vals, in_sem,
    slope, hid, msg, ext, sendb, mask, amat, amat_t, p4, p8,
    he_t, s4_t, s8_t, g8_t, hn_t, part, gath, cot_out, cot_pre, cot_g, csp, own, tmp, fsv,
    rets, ret, cot_msg, cot_pre_e,
    n_keep, n_r0s, n_r0, n_s1s, n_s1, n_ts, n_t, n_s2s, n_s2, n_s3s, n_s3, n_fs, n_f,
    u_keep, u_r0s, u_r0, u_s1s, u_s1, u_ts, u_t, u_s2s, u_s2,
    v_keep, v_r0s, v_r0, v_s1s, v_s1, v_ts, v_t, v_s2s, v_s2,
    e_s3s, e_s3,
    halo_ss, halo_rs, ret_ss, ret_rs, n_ss, n_rs, u_ss, u_rs, v_ss, v_rs, e_ss, e_rs, out_sem,
):
    R = BLK * B
    HC = H // 2
    Y = Y_LO * Y_HI
    SHARDS = Z * X * Y
    K4 = H // SHARDS
    s = lax.axis_index("stream")
    p = lax.axis_index("span")
    r = lax.axis_index("rep")
    y_lo, z = s // Z, s % Z
    y_hi, x = p // X, p % X
    y = y_hi * Y_LO + y_lo
    first = r == 0
    a = jnp.where(first, y, x)
    b = jnp.where(first, x, y)
    has = (s > 0, s < Y_LO * Z - 1, p > 0, p < Y_HI * X - 1)

    def at(yy, xx, zz):
        return {"stream": (yy % Y_LO) * Z + zz, "span": (yy // Y_LO) * X + xx, "rep": r}

    a1, a3 = a + 1 - 2 * (a % 2), 3 - a
    a2 = (a + 2) % 4

    def a_at(aa):
        return at(jnp.where(first, aa, y), jnp.where(first, x, aa), z)

    def b_peer(j):
        return at(jnp.where(first, y, (y + j) % Y), jnp.where(first, (x + j) % X, x), z)

    def z_peer(j):
        return at(y, x, (z + j) % Z)

    def across(j):
        return {**z_peer(j), "rep": 1 - r}

    partner = {"stream": s, "span": p, "rep": 1 - r}
    sides = (
        {"stream": s - 1, "span": p, "rep": r},
        {"stream": s + 1, "span": p, "rep": r},
        {"stream": s, "span": p - 1, "rep": r},
        {"stream": s, "span": p + 1, "rep": r},
    )

    def remote(src, dst, ssem, rsem, dev):
        return pltpu.make_async_remote_copy(
            src_ref=src, dst_ref=dst, send_sem=ssem, recv_sem=rsem, device_id=dev, device_id_type=MESH
        )

    pairs = (
        (st_h, st), (ew1_h, ew1), (eb1_h, eb1), (snd_h, snd_s), (ew2_h, ew2),
        (dst_h, dst_s), (src_h, src_s), (cnt_h, cnt_s), (vals_h, vals),
        (nw1_h, nw1), (nb1_h, nb1), (nw2_h, nw2), (ct_h, ct), (gain_h, gain),
    )
    loads = [pltpu.make_async_copy(src, dst, in_sem.at[i]) for i, (src, dst) in enumerate(pairs)]
    for copy in loads[:5]:
        copy.start()

    def load(*which):
        for i in which:
            loads[i].wait()

    barrier = pltpu.get_barrier_semaphore()
    peers = [a_at(a1), a_at(a3)] + [b_peer(j) for j in range(1, 4)]
    peers += [z_peer(j) for j in range(1, Z)] + [across(j) for j in range(Z)]
    for dev in peers:
        pl.semaphore_signal(barrier, inc=1, device_id=dev, device_id_type=MESH)
    halo_count = 0
    for side in range(4):
        halo_count = halo_count + has[side].astype(i32)

        @pl.when(has[side])
        def _():
            pl.semaphore_signal(barrier, inc=1, device_id=sides[side], device_id_type=MESH)

    CH = min(32, B)
    load(0, 1, 2)
    for copy in loads[5:]:
        copy.start()
    tmp[...] = mm(st[...], ew1[...])

    def edge_act(i):
        rows = pl.ds(i, CH)
        pre = tmp[rows, :] + eb1[...]
        g = jax.nn.sigmoid(pre)
        hid[rows, :] = (pre * g).astype(bf16)
        slope[rows, :] = g * (1.0 + pre * (1.0 - g))

    unrolled(R, CH, edge_act)
    load(3, 4)
    tmp[...] = mm(hid[...], ew2[...])
    for blk in range(BLK):
        msg[blk] = tmp[blk * B : (blk + 1) * B, :].astype(bf16)
    for j in range(4):
        sendb[j] = msg[snd_s[0, j]]
    pl.semaphore_wait(barrier, len(peers) + halo_count)

    back = (1, 0, 3, 2)
    halo = [
        remote(sendb.at[j], ext.at[back[j]], halo_ss.at[j], halo_rs.at[back[j]], sides[j]) for j in range(4)
    ]
    for j in range(4):

        @pl.when(has[j])
        def _():
            halo[j].start()

        @pl.when(jnp.logical_not(has[j]))
        def _():
            ext[j] = jnp.zeros((B, H), bf16)
            ret[j] = jnp.zeros((B, H), bf16)

    def masks(t, carry):
        key = jnp.where(t < cnt_s[0, 0], dst_s[0, t] * EXTENT + src_s[0, t], -1)
        keys = jnp.full((16, B), key, i32)
        for q in range(BLK * EXTENT):
            mask[t, q] = jnp.where(keys == q, 1.0, 0.0).astype(bf16)
        return carry

    load(5, 6, 7)
    lax.fori_loop(0, T, masks, 0)
    load(8)

    def tiles(i):
        rows = pl.ds(i, CH)
        totals = [jnp.zeros((CH, B), bf16)] * (BLK * EXTENT)
        for t in range(T):
            v = vals[t, rows, :]
            totals = [
                total + jnp.concatenate([mask[t, q]] * (CH // 16), axis=0) * v for q, total in enumerate(totals)
            ]
        for q, total in enumerate(totals):
            d, e = q // EXTENT, q % EXTENT
            amat[pl.ds(pl.multiple_of(d * B + i, CH), CH), e * B : (e + 1) * B] = total

    loop(B, CH, tiles)
    eye = (lax.broadcasted_iota(i32, (B, B), 0) == lax.broadcasted_iota(i32, (B, B), 1)).astype(f32).astype(bf16)
    for e in range(EXTENT):
        amat_t[e * B : (e + 1) * B, :] = nt(eye, amat[:, e * B : (e + 1) * B]).astype(bf16)

    lk, lz = log2(K4), log2(Z)
    LW = min(128, H)

    def perms(i):
        pos = i + lax.broadcasted_iota(i32, (CH, LW), 0)
        lane = lax.broadcasted_iota(i32, (CH, LW), 1)
        zz = (pos >> lk) & (Z - 1)
        bb = (pos >> (lk + lz)) & 3
        aa = (pos >> (lk + lz + 2)) & 3
        yy, xx = jnp.where(first, aa, bb), jnp.where(first, bb, aa)
        four = (((yy & 1) * Z + zz) * Y_HI + (yy >> 1)) * (X * K4) + xx * K4 + (pos & (K4 - 1))
        zz = (pos >> (lk + 1)) & (Z - 1)
        q = (pos >> (lk + 1 + lz)) & (2 * X - 1)
        yh, xx = jnp.where(first, q >> 2, q & 1), jnp.where(first, q & 3, q >> 1)
        eight = (zz * Y_HI + yh) * (2 * X * K4) + xx * (2 * K4) + (pos & (2 * K4 - 1))
        rows = pl.ds(i, CH)
        for ref, orig in ((p4, four), (p8, eight)):
            for c in range(H // LW):
                ref[rows, c * LW : (c + 1) * LW] = jnp.where(orig == lane + c * LW, 1.0, 0.0).astype(bf16)

    loop(H, CH, perms)
    he_t[...] = nt(p4[...], hid[...]).astype(bf16)
    s8_t[...] = nt(p8[...], st[...]).astype(bf16)
    load(9, 10)
    part[...] = mm(st[...], nw1[:H, :])
    own[...] = mm(amat[:, :R], msg[...].reshape(R, H))
    load(11, 12, 13)

    for j in range(4):

        @pl.when(has[j])
        def _():
            halo[back[j]].wait_recv()

    gath[...] = (own[...] + mm(amat[:, R:], ext[...].reshape(4 * B, H))).astype(bf16)
    part[...] += mm(gath[...], nw1[H:, :])

    def node_act(i):
        rows = pl.ds(i, CH)
        pre = part[rows, :] + nb1[...]
        g = jax.nn.sigmoid(pre)
        hid[rows, :] = (pre * g).astype(bf16)
        part[rows, :] = g * (1.0 + pre * (1.0 - g))

    unrolled(R, CH, node_act)
    tmp[...] = mm(hid[...], nw2[...])

    def norm(i):
        rows = pl.ds(i, CH)
        o = tmp[rows, :]
        centred = o - jnp.mean(o, axis=1, keepdims=True)
        inv = lax.rsqrt(jnp.mean(centred * centred, axis=1, keepdims=True) + norm_epsilon)
        normed = centred * inv
        fsv[rows, :] = (st[rows, :].astype(f32) + normed * gain[...]).astype(bf16)
        q = ct[rows, :].astype(f32) * gain[...]
        cot = inv * (
            q - jnp.mean(q, axis=1, keepdims=True) - normed * jnp.mean(q * normed, axis=1, keepdims=True)
        )
        cot_out[rows, :] = cot.astype(bf16)

    unrolled(R, CH, norm)
    out_fs = pltpu.make_async_copy(fsv, states_h.at[0], out_sem.at[0])
    out_fs.start()
    tmp[...] = nt(cot_out[...], nw2[...])

    def node_slope(i):
        rows = pl.ds(i, CH)
        cot_pre[rows, :] = (tmp[rows, :] * part[rows, :]).astype(bf16)

    unrolled(R, CH, node_slope)
    cot_g[...] = nt(cot_pre[...], nw1[H:, :]).astype(bf16)

    rets[...] = mm(amat_t[R:, :], cot_g[...]).astype(bf16).reshape(4, B, H)
    home = [
        remote(rets.at[g], ret.at[back[g]], ret_ss.at[g], ret_rs.at[back[g]], sides[g]) for g in range(4)
    ]
    for g in range(4):

        @pl.when(has[g])
        def _():
            home[g].start()

    hn_t[...] = nt(p4[...], hid[...]).astype(bf16)
    g8_t[...] = nt(p8[...], gath[...]).astype(bf16)
    z8, z4 = 2 * K4 * Z, K4 * Z

    def n1_grad(i):
        for y_low, left in ((0, s8_t), (1, g8_t)):
            g = mm(left[pl.ds(i, 2 * z8), :], cot_pre[...])
            sent = jnp.where(first, g[:, HC:], g[:, :HC]).astype(bf16)
            kept = jnp.where(first, g[:, :HC], g[:, HC:])
            for half in range(2):
                q = i // z8 + half
                yy = jnp.where(first, q // 4, q % 2) * 2 + y_low
                xx = jnp.where(first, q % 4, q // 2)
                aa, bb = jnp.where(first, yy, xx), jnp.where(first, xx, yy)
                block = slice(half * z8, (half + 1) * z8)
                n_keep[pl.ds(pl.multiple_of((aa * 4 + bb) * z8, z8), z8), :] = kept[block]
                n_r0s[pl.ds(pl.multiple_of((bb * 4 + aa) * z8, z8), z8), :] = sent[block]

    unrolled(H, 2 * z8, n1_grad)

    def four_rows(base, left, right, keep, send):
        def go(i):
            g = mm(left[pl.ds(i, 4 * z4), :], right[...])
            keep[pl.ds(base + i, 4 * z4), :] = jnp.where(first, g[:, :HC], g[:, HC:])
            sent = jnp.where(first, g[:, HC:], g[:, :HC]).astype(bf16)
            for bb in range(4):
                rows = pl.ds(base + bb * 4 * z4 + i // 4, z4)
                send[rows, :] = sent[bb * z4 : (bb + 1) * z4]

        unrolled(H, 4 * z4, go)

    four_rows(2 * H, hn_t, cot_out, n_keep, n_r0s)
    n_rep = remote(n_r0s, n_r0, n_ss.at[0], n_rs.at[0], partner)
    n_rep.start()
    own[...] = mm(amat_t[:R, :], cot_g[...])
    csp[...] = nt(cot_pre[...], nw1[:H, :])
    s4_t[...] = nt(p4[...], st[...]).astype(bf16)

    QC = HC // 2

    def add_partner(parts, keep, got, send):
        def go(i):
            for aa in range(4):
                off = 0
                for base, size in parts:
                    step = size // 4
                    rows = pl.ds(pl.multiple_of(base + aa * size + i * step, step), step)
                    total = (keep[rows, :] + got[rows, :].astype(f32)).astype(bf16)
                    there = pl.ds(pl.multiple_of(off + i * step, step), step)
                    send[0, aa, there, :] = total[:, :QC]
                    send[1, aa, there, :] = total[:, QC:]
                    off += size

        lax.fori_loop(0, 4, lambda i, c: (go(i), c)[1], 0)

    def first_step(send, recv, ss, rs):
        copies = []
        for half, near in ((0, a1), (1, a3)):
            for slot, chunk in ((1, a2), (0, near)):
                k = 1 + 2 * half + slot
                copies.append(
                    remote(send.at[half, chunk], recv.at[half, slot], ss.at[k], rs.at[k], a_at(near))
                )
        for copy in copies:
            copy.start()
        return copies

    def second_step(copies, send, recv, mid_s, mid_r, ss, rs):
        for copy in copies:
            copy.wait_recv()
        more = []
        for half, near in ((0, a3), (1, a1)):
            mid_s[half] = (send[half, near].astype(f32) + recv[half, 1].astype(f32)).astype(bf16)
            k = 5 + half
            copy = remote(mid_s.at[half], mid_r.at[half], ss.at[k], rs.at[k], a_at(near))
            copy.start()
            more.append(copy)
        return more

    def b_stage(copies, send, recv, mid_r, out, got, parts, ss, rs):
        for copy in copies:
            copy.wait_recv()
        for bb in range(4):
            lo = 0
            off = 0
            for size in parts:
                rows = pl.ds(lo + bb * (size // 4), size // 4)
                halves = [
                    send[h, a, rows, :].astype(f32) + recv[h, 0, rows, :].astype(f32) + mid_r[h, rows, :].astype(f32)
                    for h in range(2)
                ]
                out[bb, off : off + size // 4, :] = jnp.concatenate(halves, axis=1).astype(bf16)
                lo += size
                off += size // 4
        more = [
            remote(out.at[(b + j) % 4], got.at[j - 1], ss.at[6 + j], rs.at[6 + j], b_peer(j)) for j in (2, 1, 3)
        ]
        for copy in more:
            copy.start()
        return more

    def b_sum(copies, send, recv):
        for copy in copies:
            copy.wait_recv()
        total = send[b].astype(f32)
        for j in range(3):
            total = total + recv[j].astype(f32)
        return total

    n_parts, e_parts = ((0, 2 * H // 4), (2 * H, H // 4)), ((0, H // 4),)
    n_sizes, e_sizes = (2 * H // 4, H // 4), (H // 4,)
    k8 = 2 * K4

    n_rep.wait_recv()
    add_partner(n_parts, n_keep, n_r0, n_s1s)
    n1 = first_step(n_s1s, n_s1, n_ss, n_rs)

    for j in range(4):

        @pl.when(has[j])
        def _():
            home[back[j]].wait_recv()

    def fold(i):
        rows = pl.ds(i, CH)
        for blk in range(BLK):
            full = pl.ds(blk * B + i, CH)
            total = own[full, :]
            for j in range(4):
                total = total + jnp.where(snd_s[0, j] == blk, ret[j, rows, :].astype(f32), 0.0)
            cot_msg[full, :] = total.astype(bf16)

    unrolled(B, CH, fold)

    four_rows(0, he_t, cot_msg, u_keep, u_r0s)
    u_rep = remote(u_r0s, u_r0, u_ss.at[0], u_rs.at[0], partner)
    u_rep.start()
    n2 = second_step(n1, n_s1s, n_s1, n_ts, n_t, n_ss, n_rs)
    tmp[...] = nt(cot_msg[...], ew2[...])

    def edge_slope(i):
        rows = pl.ds(i, CH)
        cot_pre_e[rows, :] = (tmp[rows, :] * slope[rows, :]).astype(bf16)

    unrolled(R, CH, edge_slope)
    four_rows(0, s4_t, cot_pre_e, v_keep, v_r0s)
    v_rep = remote(v_r0s, v_r0, v_ss.at[0], v_rs.at[0], partner)
    v_rep.start()
    u_rep.wait_recv()
    add_partner(e_parts, u_keep, u_r0, u_s1s)
    u1 = first_step(u_s1s, u_s1, u_ss, u_rs)

    csp[...] += nt(cot_pre_e[...], ew1[...])

    def finish_state(i):
        rows = pl.ds(i, CH)
        ct[rows, :] = (ct[rows, :].astype(f32) + csp[rows, :]).astype(bf16)

    unrolled(R, CH, finish_state)
    out_sg = pltpu.make_async_copy(ct, states_h.at[1], out_sem.at[1])
    out_sg.start()

    v_rep.wait_recv()
    add_partner(e_parts, v_keep, v_r0, v_s1s)
    v1 = first_step(v_s1s, v_s1, v_ss, v_rs)

    n3 = b_stage(n2, n_s1s, n_s1, n_t, n_s2s, n_s2, n_sizes, n_ss, n_rs)
    u2 = second_step(u1, u_s1s, u_s1, u_ts, u_t, u_ss, u_rs)
    v2 = second_step(v1, v_s1s, v_s1, v_ts, v_t, v_ss, v_rs)
    u3 = b_stage(u2, u_s1s, u_s1, u_t, u_s2s, u_s2, e_sizes, u_ss, u_rs)
    v3 = b_stage(v2, v_s1s, v_s1, v_t, v_s2s, v_s2, e_sizes, v_ss, v_rs)

    rows_n = b_sum(n3, n_s2s, n_s2)
    for zz in range(Z):
        pair = z8 + (zz // 2) * k8
        n_s3s[zz] = jnp.concatenate([rows_n[zz * k8 : (zz + 1) * k8], rows_n[pair : pair + k8]], axis=0).astype(bf16)
    n4 = []
    for j in range(1, Z):
        k = 9 + j
        n4.append(remote(n_s3s.at[(z + j) % Z], n_s3.at[j - 1], n_ss.at[k], n_rs.at[k], z_peer(j)))
    for copy in n4:
        copy.start()
    rows_u = b_sum(u3, u_s2s, u_s2)
    rows_v = b_sum(v3, v_s2s, v_s2)
    for zz in range(Z):
        e_s3s[zz] = jnp.concatenate(
            [rows_v[zz * K4 : (zz + 1) * K4], rows_u[zz * K4 : (zz + 1) * K4]], axis=0
        ).astype(bf16)
    e4 = []
    for j in range(1, Z):
        e4.append(remote(e_s3s.at[(z + j) % Z], e_s3.at[0, j], e_ss.at[j], e_rs.at[j], z_peer(j)))
    for j in range(Z):
        e4.append(remote(e_s3s.at[(z + j) % Z], e_s3.at[1, j], e_ss.at[Z + j], e_rs.at[Z + j], across(j)))
    for copy in e4:
        copy.start()

    def whole(mine, theirs):
        return jnp.concatenate([jnp.where(first, mine, theirs), jnp.where(first, theirs, mine)], axis=1)

    for copy in n4:
        copy.wait_recv()
    total = n_s3s[z].astype(f32)
    for j in range(Z - 1):
        total = total + n_s3[j].astype(f32)
    n_fs[...] = total
    n_fin = remote(n_fs, n_f, n_ss.at[9 + Z], n_rs.at[9 + Z], partner)
    n_fin.start()
    n_fin.wait_recv()
    full = whole(n_fs[...], n_f[...])
    grads[:k8, :] = full[:k8]
    grads[k8 : k8 + K4, :] = jnp.where(z % 2 == 1, full[k8 + K4 :], full[k8 : k8 + K4])
    for copy in e4:
        copy.wait_recv()
    mine, theirs = e_s3s[z].astype(f32), e_s3[1, 0].astype(f32)
    for j in range(1, Z):
        mine = mine + e_s3[0, j].astype(f32)
        theirs = theirs + e_s3[1, j].astype(f32)
    grads[2 * k8 :, :] = whole(mine, theirs)

    out_fs.wait()
    out_sg.wait()
    for j in range(4):

        @pl.when(has[j])
        def _():
            halo[j].wait_send()
            home[j].wait_send()

    for copy in [n_rep, u_rep, v_rep, n_fin] + n1 + n2 + n3 + n4 + u1 + u2 + u3 + v1 + v2 + v3 + e4:
        copy.wait_send()


def deliver(K4, states_h, grads, fs_h, sg_h, ge1, ge2, gn1, gn2, buf, sem):
    into = [pltpu.make_async_copy(states_h.at[i], buf.at[i], sem.at[i]) for i in range(2)]
    out = [pltpu.make_async_copy(buf.at[i], ref, sem.at[2 + i]) for i, ref in enumerate((fs_h, sg_h))]
    for copy in into:
        copy.start()
    gn1[...] = grads[: 2 * K4, :]
    gn2[...] = grads[2 * K4 : 3 * K4, :]
    ge1[...] = grads[4 * K4 : 5 * K4, :]
    ge2[...] = grads[5 * K4 :, :]
    for i in range(2):
        into[i].wait()
        out[i].start()
    for i in range(2):
        out[i].wait()


def make_body(Z, X):
    def body(
        node_state, node_cot, edge_w1, edge_b1, edge_w2, node_w1, node_b1, node_w2, norm_gain,
        tile_dst, tile_src, tile_count, tile_vals, send_blocks,
    ):
        R, H = node_state.shape[3:]
        T, B = tile_vals.shape[2:4]
        Y = Y_LO * Y_HI
        HC = H // 2
        K4 = H // (Z * X * Y)
        k8 = 2 * K4

        def v(shape, dtype=bf16):
            return pltpu.VMEM(shape, dtype)

        def stages(total, s1, s2):
            return [
                v((total, HC), f32), v((total, HC)), v((total, HC)),
                v((2, 4, s1, HC // 2)), v((2, 2, s1, HC // 2)), v((2, s1, HC // 2)), v((2, s1, HC // 2)),
                v((4, s2, HC)), v((3, s2, HC)),
            ]

        dma = pltpu.SemaphoreType.DMA
        scratch = [pltpu.SMEM((1, T), i32), pltpu.SMEM((1, T), i32), pltpu.SMEM((1, 1), i32), pltpu.SMEM((1, 4), i32)]
        scratch += [v((1, H), f32)] * 3
        scratch += [
            v((R, H)), v((R, H)), v((H, H)), v((H, H)), v((2 * H, H)), v((H, H)), v((T, B, B)), dma((14,)),
            v((R, H), f32), v((R, H)), v((BLK, B, H)), v((4, B, H)), v((4, B, H)), v((T, BLK * EXTENT, 16, B)),
            v((R, EXTENT * B)), v((EXTENT * B, R)), v((H, H)), v((H, H)),
            v((H, R)), v((H, R)), v((H, R)), v((H, R)), v((H, R)), v((R, H), f32), v((R, H)), v((R, H)), v((R, H)),
            v((R, H)), v((R, H), f32), v((R, H), f32), v((R, H), f32), v((R, H)),
            v((4, B, H)), v((4, B, H)), v((R, H)), v((R, H)),
        ]
        scratch += stages(3 * H, 3 * H // 4, 3 * H // 16)
        scratch += [v((Z, 2 * k8, HC)), v((Z - 1, 2 * k8, HC)), v((2 * k8, HC), f32), v((2 * k8, HC), f32)]
        scratch += stages(H, H // 4, H // 16) * 2
        scratch += [v((Z, k8, HC)), v((2, Z, k8, HC))]
        scratch += [dma((4,))] * 4 + [dma((10 + Z,))] * 2 + [dma((10,))] * 4 + [dma((2 * Z,))] * 2 + [dma((2,))]
        vmem = pl.BlockSpec(memory_space=pltpu.VMEM)
        hbm = pl.BlockSpec(memory_space=pl.ANY)
        states, grads = pl.pallas_call(
            functools.partial(kernel, Z, X, H, B, T),
            out_shape=(jax.ShapeDtypeStruct((2, R, H), bf16), jax.ShapeDtypeStruct((6 * K4, H), f32)),
            in_specs=[hbm] * 14,
            out_specs=(hbm, vmem),
            scratch_shapes=scratch,
            compiler_params=pltpu.CompilerParams(
                collective_id=0, has_side_effects=True, vmem_limit_bytes=60 * 1024 * 1024
            ),
            name="step",
        )(
            tile_dst.reshape(1, T), tile_src.reshape(1, T), tile_count, send_blocks.reshape(1, 4),
            edge_b1.reshape(1, H), node_b1.reshape(1, H), norm_gain.reshape(1, H),
            node_state.reshape(R, H), node_cot.reshape(R, H), edge_w1.reshape(H, H), edge_w2.reshape(H, H),
            node_w1.reshape(2 * H, H), node_w2.reshape(H, H), tile_vals.reshape(T, B, B),
        )
        outs = pl.pallas_call(
            functools.partial(deliver, K4),
            out_shape=(
                jax.ShapeDtypeStruct((R, H), bf16),
                jax.ShapeDtypeStruct((R, H), bf16),
                jax.ShapeDtypeStruct((K4, H), f32),
                jax.ShapeDtypeStruct((K4, H), f32),
                jax.ShapeDtypeStruct((k8, H), f32),
                jax.ShapeDtypeStruct((K4, H), f32),
            ),
            in_specs=[hbm, vmem],
            out_specs=[hbm] * 2 + [vmem] * 4,
            scratch_shapes=[v((2, R, H)), dma((4,))],
            name="deliver",
        )(states, grads)
        return (outs[0].reshape(node_state.shape), outs[1].reshape(node_state.shape)) + tuple(outs[2:])

    return body


def solution(mesh):
    in_specs = (
        P("rep", "stream", "span", None, None),
        P("rep", "stream", "span", None, None),
        P(), P(), P(), P(), P(), P(), P(),
        P("stream", "span", None),
        P("stream", "span", None),
        P("stream", "span"),
        P("stream", "span", None, None, None),
        P("stream", "span", None, None),
    )
    out_specs = (
        P("rep", "stream", "span", None, None),
        P("rep", "stream", "span", None, None),
        P(("stream", "span"), None),
        P(("stream", "span"), None),
        P(("stream", "span"), None),
        P(("stream", "span"), None),
    )
    body = make_body(mesh.shape["stream"] // Y_LO, mesh.shape["span"] // Y_HI)
    return jax.shard_map(body, mesh=mesh, in_specs=in_specs, out_specs=out_specs, check_vma=False)
```

time: 61.1 us -> 52.7 us (0.86)
  local copies, waits for them, and re-layouts: 5.08 us -> 0 us
  Pallas kernels: 54.6 us -> 51.2 us
    pallas_call x1, Pallas kernels: 54.6 us -> 47.9 us  [body(): pl.pallas_call(functools.partial(kernel, Z, X, H, B, T), out_shape=(jax.S...]
    unnamed x16 -> x0, local copies, waits for them, and re-layouts: 5.08 us -> none
    pallas_call x0 -> x1, Pallas kernels: none -> 3.32 us  [body(): pl.pallas_call(functools.partial(deliver, K4), out_shape=(jax.ShapeDtypeS...]
where the time goes in v2:
time: 52.7 us; the launch traced here: 52.5 us
  Pallas kernels  51.2 us (97%)
  between operations  1.29 us (2%)
    pallas_call x1, Pallas kernels, body(): pl.pallas_call(functools.partial(kernel, Z, X, H, B, T), out_shape=(jax.S...  47.9 us
    pallas_call x1, Pallas kernels, body(): pl.pallas_call(functools.partial(deliver, K4), out_shape=(jax.ShapeDtypeS...  3.32 us

profile of v2, /device:TPU:1, one launch (start us, length us, event | category | flops | bytes accessed | tf_op | source)
XLA Modules:
  0.0 52.5 jit_solution(2947694343029930381)
XLA Ops:
  1.3 47.9 %step.1 = (bf16[2,384,512]{2,1,0:T(8,128)(2,1)}, f32[24,512]{1,0:T(8,128)}) custom-call(s32[1,24]{1,0:T(1,128)} %bitcast.19, s32[1,24]{1,0:T(1,128)} %bitcast.20, s32[1,1]{1,0:T(1,128)S(6)} %copy.20.cnt_h, s32[1,4]{1,0:T(1,128)} %bitcast.21, f32[1,512]{1,0:T(1,128)} %eb1_h.1, f32[1,512]{1,0:T(1,128)} %nb1_h.1, f32[1,512]{1,0:T(1,128)} %gain_h.1, ...), custom_call_target="tpu_custom_call" | custom-call | tf_op jit(solution)/shard_map/step/pallas_call | solution.py:569
  49.2 3.3 %deliver.1 = (bf16[384,512]{1,0:T(8,128)(2,1)}, bf16[384,512]{1,0:T(8,128)(2,1)}, f32[4,512]{1,0:T(4,128)}, f32[4,512]{1,0:T(4,128)}, f32[8,512]{1,0:T(8,128)}, /*index=5*/f32[4,512]{1,0:T(4,128)}) custom-call(bf16[2,384,512]{2,1,0:T(8,128)(2,1)} %get-tuple-element.14.states_h, f32[24,512]{1,0:T(8,128)} %get-tuple-element.15.grads), custom_call_target="tpu_custom_call" | custom-call | tf_op jit(solution)/shard_map/deliver/pallas_call | solution.py:585

commit v3 on v2

--- a/solution.py
+++ b/solution.py
@@ -510,20 +510,20 @@
         copy.wait_send()
 
 
-def deliver(K4, states_h, grads, fs_h, sg_h, ge1, ge2, gn1, gn2, buf, sem):
-    into = [pltpu.make_async_copy(states_h.at[i], buf.at[i], sem.at[i]) for i in range(2)]
-    out = [pltpu.make_async_copy(buf.at[i], ref, sem.at[2 + i]) for i, ref in enumerate((fs_h, sg_h))]
-    for copy in into:
+def deliver(K4, states, grads, fs_h, sg_h, ge1_h, ge2_h, gn1_h, gn2_h, ge1, ge2, gn1, gn2, sem):
+    out = [pltpu.make_async_copy(states.at[i], ref, sem.at[i]) for i, ref in enumerate((fs_h, sg_h))]
+    for copy in out:
         copy.start()
     gn1[...] = grads[: 2 * K4, :]
     gn2[...] = grads[2 * K4 : 3 * K4, :]
     ge1[...] = grads[4 * K4 : 5 * K4, :]
     ge2[...] = grads[5 * K4 :, :]
-    for i in range(2):
-        into[i].wait()
-        out[i].start()
-    for i in range(2):
-        out[i].wait()
+    for i, (src, dst) in enumerate(((gn1, gn1_h), (gn2, gn2_h), (ge1, ge1_h), (ge2, ge2_h))):
+        copy = pltpu.make_async_copy(src, dst, sem.at[2 + i])
+        copy.start()
+        out.append(copy)
+    for copy in out:
+        copy.wait()
 
 
 def make_body(Z, X):
@@ -565,22 +565,29 @@
         scratch += [v((Z, k8, HC)), v((2, Z, k8, HC))]
         scratch += [dma((4,))] * 4 + [dma((10 + Z,))] * 2 + [dma((10,))] * 4 + [dma((2 * Z,))] * 2 + [dma((2,))]
         vmem = pl.BlockSpec(memory_space=pltpu.VMEM)
-        hbm = pl.BlockSpec(memory_space=pl.ANY)
+        hbm = pl.BlockSpec(memory_space=pltpu.HBM)
+        anywhere = pl.BlockSpec(memory_space=pl.ANY)
+        inputs = (
+            tile_dst.reshape(1, T), tile_src.reshape(1, T), tile_count, send_blocks.reshape(1, 4),
+            edge_b1.reshape(1, H), node_b1.reshape(1, H), norm_gain.reshape(1, H),
+            node_state.reshape(R, H), node_cot.reshape(R, H), edge_w1.reshape(H, H), edge_w2.reshape(H, H),
+            node_w1.reshape(2 * H, H), node_w2.reshape(H, H), tile_vals.reshape(T, B, B),
+        )
+        inputs = [
+            array if i == 2 else pltpu.with_memory_space_constraint(array, pltpu.HBM) for i, array in enumerate(inputs)
+        ]
         states, grads = pl.pallas_call(
             functools.partial(kernel, Z, X, H, B, T),
             out_shape=(jax.ShapeDtypeStruct((2, R, H), bf16), jax.ShapeDtypeStruct((6 * K4, H), f32)),
             in_specs=[hbm] * 14,
-            out_specs=(hbm, vmem),
+            out_specs=(anywhere, vmem),
             scratch_shapes=scratch,
             compiler_params=pltpu.CompilerParams(
-                collective_id=0, has_side_effects=True, vmem_limit_bytes=60 * 1024 * 1024
+                collective_id=0, has_side_effects=True, vmem_limit_bytes=40 * 1024 * 1024
             ),
             name="step",
         )(
-            tile_dst.reshape(1, T), tile_src.reshape(1, T), tile_count, send_blocks.reshape(1, 4),
-            edge_b1.reshape(1, H), node_b1.reshape(1, H), norm_gain.reshape(1, H),
-            node_state.reshape(R, H), node_cot.reshape(R, H), edge_w1.reshape(H, H), edge_w2.reshape(H, H),
-            node_w1.reshape(2 * H, H), node_w2.reshape(H, H), tile_vals.reshape(T, B, B),
+            *inputs
         )
         outs = pl.pallas_call(
             functools.partial(deliver, K4),
@@ -592,9 +599,10 @@
                 jax.ShapeDtypeStruct((k8, H), f32),
                 jax.ShapeDtypeStruct((K4, H), f32),
             ),
-            in_specs=[hbm, vmem],
-            out_specs=[hbm] * 2 + [vmem] * 4,
-            scratch_shapes=[v((2, R, H)), dma((4,))],
+            in_specs=[anywhere, vmem],
+            out_specs=[hbm] * 6,
+            scratch_shapes=[v((rows, H), f32) for rows in (K4, K4, k8, K4)] + [dma((6,))],
+            compiler_params=pltpu.CompilerParams(vmem_limit_bytes=4 * 1024 * 1024),
             name="deliver",
         )(states, grads)
         return (outs[0].reshape(node_state.shape), outs[1].reshape(node_state.shape)) + tuple(outs[2:])

time: 52.7 us -> 49.9 us (0.947)
  Pallas kernels: 51.2 us -> 48.5 us
    pallas_call x1, Pallas kernels: 3.32 us -> 0.94 us  [body(): pl.pallas_call(functools.partial(deliver, K4), out_shape=(jax.ShapeDtypeS...]
where the time goes in v3:
time: 49.9 us; the launch traced here: 49.8 us
  Pallas kernels  48.5 us (97%)
  between operations  1.29 us (3%)
    pallas_call x1, Pallas kernels, body(): pl.pallas_call(functools.partial(kernel, Z, X, H, B, T), out_shape=(jax.S...  47.6 us

profile of v3, /device:TPU:1, one launch (start us, length us, event | category | flops | bytes accessed | tf_op | source)
XLA Modules:
  0.0 49.8 jit_solution(16857166986431748140)
XLA Ops:
  1.3 47.6 %step.1 = (bf16[2,384,512]{2,1,0:T(8,128)(2,1)S(1)}, f32[24,512]{1,0:T(8,128)S(1)}) custom-call(s32[1,24]{1,0:T(1,128)} %bitcast.19, s32[1,24]{1,0:T(1,128)} %bitcast.20, s32[1,1]{1,0:T(1,128)S(6)} %copy.20.cnt_h, s32[1,4]{1,0:T(1,128)} %bitcast.21, f32[1,512]{1,0:T(1,128)} %eb1_h.1, f32[1,512]{1,0:T(1,128)} %nb1_h.1, f32[1,512]{1,0:T(1,128)} %gain_h.1, ...), custom_call_target="tpu_custom_call" | custom-call | tf_op jit(solution)/shard_map/step/pallas_call | solution.py:579
  48.9 0.9 %deliver.1 = (bf16[384,512]{1,0:T(8,128)(2,1)}, bf16[384,512]{1,0:T(8,128)(2,1)}, f32[4,512]{1,0:T(4,128)}, f32[4,512]{1,0:T(4,128)}, f32[8,512]{1,0:T(8,128)}, /*index=5*/f32[4,512]{1,0:T(4,128)}) custom-call(bf16[2,384,512]{2,1,0:T(8,128)(2,1)S(1)} %get-tuple-element.14.states, f32[24,512]{1,0:T(8,128)S(1)} %get-tuple-element.15.grads), custom_call_target="tpu_custom_call" | custom-call | tf_op jit(solution)/shard_map/deliver/pallas_call | solution.py:592

commit v4 on v3

--- a/solution.py
+++ b/solution.py
@@ -142,7 +142,7 @@
         pre = tmp[rows, :] + eb1[...]
         g = jax.nn.sigmoid(pre)
         hid[rows, :] = (pre * g).astype(bf16)
-        slope[rows, :] = g * (1.0 + pre * (1.0 - g))
+        slope[rows, :] = pre
 
     unrolled(R, CH, edge_act)
     load(3, 4)
@@ -217,6 +217,13 @@
                 ref[rows, c * LW : (c + 1) * LW] = jnp.where(orig == lane + c * LW, 1.0, 0.0).astype(bf16)
 
     loop(H, CH, perms)
+    def to_slope(i):
+        rows = pl.ds(i, CH)
+        pre = slope[rows, :]
+        g = jax.nn.sigmoid(pre)
+        slope[rows, :] = g * (1.0 + pre * (1.0 - g))
+
+    unrolled(R, CH, to_slope)
     he_t[...] = nt(p4[...], hid[...]).astype(bf16)
     s8_t[...] = nt(p8[...], st[...]).astype(bf16)
     load(9, 10)
@@ -393,13 +400,14 @@
 
     n_rep.wait_recv()
     add_partner(n_parts, n_keep, n_r0, n_s1s)
-    n1 = first_step(n_s1s, n_s1, n_ss, n_rs)
 
     for j in range(4):
 
         @pl.when(has[j])
         def _():
             home[back[j]].wait_recv()
+
+    n1 = first_step(n_s1s, n_s1, n_ss, n_rs)
 
     def fold(i):
         rows = pl.ds(i, CH)
@@ -415,7 +423,6 @@
     four_rows(0, he_t, cot_msg, u_keep, u_r0s)
     u_rep = remote(u_r0s, u_r0, u_ss.at[0], u_rs.at[0], partner)
     u_rep.start()
-    n2 = second_step(n1, n_s1s, n_s1, n_ts, n_t, n_ss, n_rs)
     tmp[...] = nt(cot_msg[...], ew2[...])
 
     def edge_slope(i):
@@ -443,10 +450,10 @@
     v_rep.wait_recv()
     add_partner(e_parts, v_keep, v_r0, v_s1s)
     v1 = first_step(v_s1s, v_s1, v_ss, v_rs)
-
-    n3 = b_stage(n2, n_s1s, n_s1, n_t, n_s2s, n_s2, n_sizes, n_ss, n_rs)
+    n2 = second_step(n1, n_s1s, n_s1, n_ts, n_t, n_ss, n_rs)
     u2 = second_step(u1, u_s1s, u_s1, u_ts, u_t, u_ss, u_rs)
     v2 = second_step(v1, v_s1s, v_s1, v_ts, v_t, v_ss, v_rs)
+    n3 = b_stage(n2, n_s1s, n_s1, n_t, n_s2s, n_s2, n_sizes, n_ss, n_rs)
     u3 = b_stage(u2, u_s1s, u_s1, u_t, u_s2s, u_s2, e_sizes, u_ss, u_rs)
     v3 = b_stage(v2, v_s1s, v_s1, v_t, v_s2s, v_s2, e_sizes, v_ss, v_rs)
 

time: 49.9 us -> 49.9 us (level)
  no operation moved by 1% of the time
where the time goes in v4:
time: 49.9 us; the launch traced here: 49.7 us
  Pallas kernels  48.4 us (97%)
  between operations  1.29 us (3%)
    pallas_call x1, Pallas kernels, body(): pl.pallas_call(functools.partial(kernel, Z, X, H, B, T), out_shape=(jax.S...  47.5 us

profile of v4, /device:TPU:1, one launch (start us, length us, event | category | flops | bytes accessed | tf_op | source)
XLA Modules:
  0.0 49.7 jit_solution(5820137013816508465)
XLA Ops:
  1.3 47.5 %step.1 = (bf16[2,384,512]{2,1,0:T(8,128)(2,1)S(1)}, f32[24,512]{1,0:T(8,128)S(1)}) custom-call(s32[1,24]{1,0:T(1,128)} %bitcast.19, s32[1,24]{1,0:T(1,128)} %bitcast.20, s32[1,1]{1,0:T(1,128)S(6)} %copy.20.cnt_h, s32[1,4]{1,0:T(1,128)} %bitcast.21, f32[1,512]{1,0:T(1,128)} %eb1_h.1, f32[1,512]{1,0:T(1,128)} %nb1_h.1, f32[1,512]{1,0:T(1,128)} %gain_h.1, ...), custom_call_target="tpu_custom_call" | custom-call | tf_op jit(solution)/shard_map/step/pallas_call | solution.py:586
  48.8 0.9 %deliver.1 = (bf16[384,512]{1,0:T(8,128)(2,1)}, bf16[384,512]{1,0:T(8,128)(2,1)}, f32[4,512]{1,0:T(4,128)}, f32[4,512]{1,0:T(4,128)}, f32[8,512]{1,0:T(8,128)}, /*index=5*/f32[4,512]{1,0:T(4,128)}) custom-call(bf16[2,384,512]{2,1,0:T(8,128)(2,1)S(1)} %get-tuple-element.14.states, f32[24,512]{1,0:T(8,128)S(1)} %get-tuple-element.15.grads), custom_call_target="tpu_custom_call" | custom-call | tf_op jit(solution)/shard_map/deliver/pallas_call | solution.py:599

commit v5 on v4

--- a/solution.py
+++ b/solution.py
@@ -51,7 +51,7 @@
     st, ct, ew1, ew2, nw1, nw2, vals, in_sem,
     slope, hid, msg, ext, sendb, mask, amat, amat_t, p4, p8,
     he_t, s4_t, s8_t, g8_t, hn_t, part, gath, cot_out, cot_pre, cot_g, csp, own, tmp, fsv,
-    rets, ret, cot_msg, cot_pre_e,
+    rets, ret, fsel, cot_msg, cot_pre_e,
     n_keep, n_r0s, n_r0, n_s1s, n_s1, n_ts, n_t, n_s2s, n_s2, n_s3s, n_s3, n_fs, n_f,
     u_keep, u_r0s, u_r0, u_s1s, u_s1, u_ts, u_t, u_s2s, u_s2,
     v_keep, v_r0s, v_r0, v_s1s, v_s1, v_ts, v_t, v_s2s, v_s2,
@@ -322,6 +322,11 @@
     own[...] = mm(amat_t[:R, :], cot_g[...])
     csp[...] = nt(cot_pre[...], nw1[:H, :])
     s4_t[...] = nt(p4[...], st[...]).astype(bf16)
+    for j in range(4):
+        for blk in range(BLK):
+            fsel[blk * B : (blk + 1) * B, j * B : (j + 1) * B] = jnp.where(
+                snd_s[0, j] == blk, eye.astype(f32), 0.0
+            ).astype(bf16)
 
     QC = HC // 2
 
@@ -409,16 +414,7 @@
 
     n1 = first_step(n_s1s, n_s1, n_ss, n_rs)
 
-    def fold(i):
-        rows = pl.ds(i, CH)
-        for blk in range(BLK):
-            full = pl.ds(blk * B + i, CH)
-            total = own[full, :]
-            for j in range(4):
-                total = total + jnp.where(snd_s[0, j] == blk, ret[j, rows, :].astype(f32), 0.0)
-            cot_msg[full, :] = total.astype(bf16)
-
-    unrolled(B, CH, fold)
+    cot_msg[...] = (own[...] + mm(fsel[...], ret[...].reshape(4 * B, H))).astype(bf16)
 
     four_rows(0, he_t, cot_msg, u_keep, u_r0s)
     u_rep = remote(u_r0s, u_r0, u_ss.at[0], u_rs.at[0], partner)
@@ -496,6 +492,17 @@
     full = whole(n_fs[...], n_f[...])
     grads[:k8, :] = full[:k8]
     grads[k8 : k8 + K4, :] = jnp.where(z % 2 == 1, full[k8 + K4 :], full[k8 : k8 + K4])
+    out_fs.wait()
+    out_sg.wait()
+    for j in range(4):
+
+        @pl.when(has[j])
+        def _():
+            halo[j].wait_send()
+            home[j].wait_send()
+
+    for copy in [n_rep, u_rep, v_rep, n_fin] + n1 + n2 + n3 + n4 + u1 + u2 + u3 + v1 + v2 + v3:
+        copy.wait_send()
     for copy in e4:
         copy.wait_recv()
     mine, theirs = e_s3s[z].astype(f32), e_s3[1, 0].astype(f32)
@@ -504,16 +511,7 @@
         theirs = theirs + e_s3[1, j].astype(f32)
     grads[2 * k8 :, :] = whole(mine, theirs)
 
-    out_fs.wait()
-    out_sg.wait()
-    for j in range(4):
-
-        @pl.when(has[j])
-        def _():
-            halo[j].wait_send()
-            home[j].wait_send()
-
-    for copy in [n_rep, u_rep, v_rep, n_fin] + n1 + n2 + n3 + n4 + u1 + u2 + u3 + v1 + v2 + v3 + e4:
+    for copy in e4:
         copy.wait_send()
 
 
@@ -564,7 +562,7 @@
             v((R, EXTENT * B)), v((EXTENT * B, R)), v((H, H)), v((H, H)),
             v((H, R)), v((H, R)), v((H, R)), v((H, R)), v((H, R)), v((R, H), f32), v((R, H)), v((R, H)), v((R, H)),
             v((R, H)), v((R, H), f32), v((R, H), f32), v((R, H), f32), v((R, H)),
-            v((4, B, H)), v((4, B, H)), v((R, H)), v((R, H)),
+            v((4, B, H)), v((4, B, H)), v((R, 4 * B)), v((R, H)), v((R, H)),
         ]
         scratch += stages(3 * H, 3 * H // 4, 3 * H // 16)
         scratch += [v((Z, 2 * k8, HC)), v((Z - 1, 2 * k8, HC)), v((2 * k8, HC), f32), v((2 * k8, HC), f32)]

time: 49.9 us -> 49.8 us (level)
  no operation moved by 1% of the time
where the time goes in v5:
time: 49.8 us; the launch traced here: 49.7 us
  Pallas kernels  48.4 us (97%)
  between operations  1.29 us (3%)
    pallas_call x1, Pallas kernels, body(): pl.pallas_call(functools.partial(kernel, Z, X, H, B, T), out_shape=(jax.S...  47.5 us

profile of v5, /device:TPU:1, one launch (start us, length us, event | category | flops | bytes accessed | tf_op | source)
XLA Modules:
  0.0 49.7 jit_solution(1707764179180677797)
XLA Ops:
  1.3 47.5 %step.1 = (bf16[2,384,512]{2,1,0:T(8,128)(2,1)S(1)}, f32[24,512]{1,0:T(8,128)S(1)}) custom-call(s32[1,24]{1,0:T(1,128)} %bitcast.19, s32[1,24]{1,0:T(1,128)} %bitcast.20, s32[1,1]{1,0:T(1,128)S(6)} %copy.20.cnt_h, s32[1,4]{1,0:T(1,128)} %bitcast.21, f32[1,512]{1,0:T(1,128)} %eb1_h.1, f32[1,512]{1,0:T(1,128)} %nb1_h.1, f32[1,512]{1,0:T(1,128)} %gain_h.1, ...), custom_call_target="tpu_custom_call" | custom-call | tf_op jit(solution)/shard_map/step/pallas_call | solution.py:584
  48.8 0.9 %deliver.1 = (bf16[384,512]{1,0:T(8,128)(2,1)}, bf16[384,512]{1,0:T(8,128)(2,1)}, f32[4,512]{1,0:T(4,128)}, f32[4,512]{1,0:T(4,128)}, f32[8,512]{1,0:T(8,128)}, /*index=5*/f32[4,512]{1,0:T(4,128)}) custom-call(bf16[2,384,512]{2,1,0:T(8,128)(2,1)S(1)} %get-tuple-element.14.states, f32[24,512]{1,0:T(8,128)S(1)} %get-tuple-element.15.grads), custom_call_target="tpu_custom_call" | custom-call | tf_op jit(solution)/shard_map/deliver/pallas_call | solution.py:597
